TPU v7x, 32 devices: a whole 2x2x4 slice. The times are simulated.
32 devices in a mesh: wide: 8 (over z, x), narrow: 4 (over y, core).
Axes of the slice: x: 2, y: 2, z: 4, core: 2. Of those that a mesh axis runs over, the one named last changes fastest.
Arguments:
- tiles: bfloat16 [4, 64, 2048, 128], P(None, None, ('wide', 'narrow')), may hold values from -4 to 4
- slot: int32 [32, 4], P(('wide', 'narrow')), may hold values from 0 to 3, each once within a row
- a_factor: float32 [2048, 256], P(('wide', 'narrow')), may hold values from -1.6 to 1.6
- b_factor: float32 [1024, 256], P('wide'), may hold values from -1.6 to 1.6
- c_factor: float32 [512, 256], P('wide'), may hold values from -1.6 to 1.6
- a_velocity: float32 [2048, 256], P(('wide', 'narrow')), may hold values from -0.012 to 0.012
- b_velocity: float32 [1024, 256], P('wide'), may hold values from -0.012 to 0.012
- c_velocity: float32 [512, 256], P('wide'), may hold values from -0.012 to 0.012
Outputs:
- a_out: float32 [2048, 256], P(('wide', 'narrow'))
- b_out: float32 [1024, 256], P('wide')
- c_out: float32 [512, 256], P('wide')
Inputs may be any that keep to these rules, and one draw needn't show every extreme that they name: Each row of slot names every one of the 4 tiles of its row block once.
All inputs are finite; a program needn't handle non-finite values.
Results may differ from a plain program's by a relative error of at most 0.0003.
Values sent between devices are 32-bit elements; how exact they have to be, the bound alone decides.
No kernel may reach another device: no remote copies, remote signals or barrier semaphores. Data moves between devices by JAX's collectives and lax.ppermute only.
A program may use at most 64 MiB of HBM per device.

v0:
```python
import functools

import jax
import jax.numpy as jnp
from jax import lax
from jax.experimental import pallas as pl
from jax.experimental.pallas import tpu as pltpu
from jax.sharding import PartitionSpec as P


STRATA = 4
SECOND_STRIDE = 1
THIRD_STRIDE = 3
CORES = 2
STEP = 8

momentum = 0.9
step_rate = 20.0

BOTH = ("wide", "narrow")
GRANT = pltpu.CompilerParams(vmem_limit_bytes=20 << 20)
HBM = pl.BlockSpec(memory_space=pltpu.HBM)
VMEM = pl.BlockSpec(memory_space=pltpu.VMEM)
SMEM = pl.BlockSpec(memory_space=pltpu.SMEM)


def f32(*shape):
    return jax.ShapeDtypeStruct(shape, jnp.float32)


def in_hbm(x):
    return pltpu.with_memory_space_constraint(x, pltpu.HBM)


def halves(x):
    hi = x.astype(jnp.bfloat16)
    lo = (x - hi.astype(jnp.float32)).astype(jnp.bfloat16)
    return hi, lo


def dot(x, y, contract=((1,), (0,))):
    return lax.dot_general(x, y, (contract, ((), ())), preferred_element_type=jnp.float32)


def gram(x):
    hi, lo = halves(x)
    return dot(
        jnp.concatenate([hi, hi, lo], axis=0), jnp.concatenate([hi, lo, hi], axis=0), ((0,), (0,))
    )


def apply(x, g):
    xh, xl = halves(x)
    gh, gl = halves(g)
    return dot(xh, gh) + (dot(xh, gl) + dot(xl, gh))


def doubled(x):
    return jnp.concatenate([x, x], axis=1)


def split_rows(x):
    return jnp.concatenate(halves(x), axis=0)


def pair_weights(a):
    hi, lo = halves(a)
    zero = jnp.zeros_like(hi)
    left = jnp.concatenate([hi, zero, lo, zero], axis=0)
    right = jnp.concatenate([zero, hi, zero, lo], axis=0)
    return jnp.concatenate([left, right], axis=1)


def products(tile, at, weights):
    _, ib, jb = tile.shape
    rank = weights.shape[1] // 2
    turned = [tile[pl.ds(at + m, 2)].reshape(2 * ib, jb).T for m in range(0, STEP, 2)]
    z = dot(doubled(jnp.concatenate(turned, axis=0)), weights)
    return [z[m // 2 * jb : (m // 2 + 1) * jb, m % 2 * rank : (m % 2 + 1) * rank] for m in range(STEP)]


def slices_times_b(tile, at, stacked):
    _, ib, jb = tile.shape
    x = tile[pl.ds(at, STEP)].reshape(STEP * ib, jb)
    return dot(doubled(x), stacked).reshape(STEP, ib, stacked.shape[1])


def advance_a(tile, a, va, b, c, bc_gram, scale):
    kb, ib, _ = tile.shape
    stacked = split_rows(b[...])

    def body(n, acc):
        at = pl.multiple_of(n * STEP, STEP)
        y = slices_times_b(tile, at, stacked)
        cs = c[pl.ds(at, STEP), :]
        for m in range(STEP):
            acc = acc + y[m] * cs[m : m + 1]
        return acc

    seen = lax.fori_loop(0, kb // STEP, body, jnp.zeros((ib, a.shape[1]), jnp.float32), unroll=2)
    grad = apply(a[...], bc_gram[...]) - seen
    va_new = momentum * va[...] + grad * scale
    return a[...] - step_rate * va_new, va_new


def window_kernel(slot, tiles, old, a, va, b, c, bc_gram, new, a_out, va_out, ata, z, sem, *, scale, stratum):
    copy = pltpu.make_async_copy(tiles.at[slot[0, stratum]], new, sem)
    copy.start()
    a_new, va_new = advance_a(old, a, va, b, c, bc_gram, scale)
    a_out[...] = a_new
    va_out[...] = va_new
    ata[...] = gram(a_new)
    weights = pair_weights(a_new)
    copy.wait()

    def body(n, carry):
        at = pl.multiple_of(n * STEP, STEP)
        for m, zk in enumerate(products(new, at, weights)):
            z[at + m] = zk
        return carry

    lax.fori_loop(0, new.shape[0] // STEP, body, 0, unroll=2)


def last_kernel(old, a, va, b, c, bc_gram, a_out, *, scale):
    a_out[...] = advance_a(old, a, va, b, c, bc_gram, scale)[0]


def place(core, for_b, for_c, keep, send):
    half = for_b.shape[0] // CORES
    keep[half:] = for_c
    send[half:] = for_c

    @pl.when(core[0] == 0)
    def _():
        keep[:half] = for_b[:half]
        send[:half] = for_b[half:]

    @pl.when(core[0] != 0)
    def _():
        keep[:half] = for_b[half:]
        send[:half] = for_b[:half]


def first_kernel(
    core, slot, tiles, a_in, b_in, c_in, va_in, vb_in, vc_in, tile, a, b, c, va, bc_gram, keep, send,
    vb, vc, mb, mc, tile_sem, sem, *, mult_b, mult_c, chips,
):
    kb, _, jb = tile.shape
    rank = a.shape[1]
    chunks = tile_sem.shape[0]
    size = kb // chunks
    pairs = [(a_in, a), (b_in, b), (c_in, c), (va_in, va), (vb_in, vb), (vc_in, vc)]
    rest = [pltpu.make_async_copy(x, y, sem.at[n]) for n, (x, y) in enumerate(pairs)]
    for copy in rest:
        copy.start()
    source = tiles.at[slot[0, 0]]
    parts = [
        pltpu.make_async_copy(source.at[pl.ds(n * size, size)], tile.at[pl.ds(n * size, size)], tile_sem.at[n])
        for n in range(chunks)
    ]
    for copy in parts:
        copy.start()
    for copy in rest:
        copy.wait()
    a_gram = gram(a[...])
    drag = momentum * step_rate
    lead = jnp.where(core[0] == 0, 1.0 / chips, 0.0)
    b_gram, c_gram = gram(b[...]), gram(c[...])
    bc_gram[...] = b_gram * c_gram
    mb[...] = lead * (b[...] - drag * vb[...]) - mult_b * apply(b[...], a_gram * c_gram)
    base_c = (1.0 / chips - lead) * (c[...] - drag * vc[...]) - mult_c * apply(c[...], a_gram * b_gram)
    weights = pair_weights(a[...])

    def body(n, acc):
        at = pl.multiple_of(n * STEP, STEP)
        cs = c[pl.ds(at, STEP), :]
        rows = []
        for m, zk in enumerate(products(tile, at, weights)):
            acc = acc + zk * cs[m : m + 1]
            rows.append(jnp.sum(zk * b[...], axis=0, keepdims=True))
        mc[pl.ds(at, STEP), :] = jnp.concatenate(rows, axis=0)
        return acc

    acc = jnp.zeros((jb, rank), jnp.float32)
    for n, copy in enumerate(parts):
        copy.wait()
        acc = lax.fori_loop(n * size // STEP, (n + 1) * size // STEP, body, acc)
    place(core, mb[...] + mult_b * acc, base_c + mult_c * mc[...], keep, send)


def gradient_kernel(core, tile, z, a, ata, mine, other, b, c, now, bc_gram, keep, send, mb, mc, *, mult_b, mult_c):
    kb, jb, rank = z.shape
    half = jb // CORES
    first = core[0] == 0

    @pl.when(first)
    def _():
        b[:half] = mine[:half]
        b[half:] = other[:half]

    @pl.when(jnp.logical_not(first))
    def _():
        b[:half] = other[:half]
        b[half:] = mine[:half]

    c[...] = mine[half:] + other[half:]

    @pl.when(first)
    def _():
        now[...] = b[...]

    @pl.when(jnp.logical_not(first))
    def _():
        now[...] = jnp.zeros(now.shape, jnp.float32)
        now[:kb] = c[...]

    stacked = split_rows(b[...])
    a_rows = a[...]
    mb[...] = jnp.zeros((jb, rank), jnp.float32)

    def body(n, carry):
        at = pl.multiple_of(n * STEP, STEP)
        y = slices_times_b(tile, at, stacked)
        mc[pl.ds(at, STEP), :] = jnp.concatenate(
            [jnp.sum(y[m] * a_rows, axis=0, keepdims=True) for m in range(STEP)], axis=0
        )
        cs = c[pl.ds(at, STEP), :]
        for lo in range(0, jb, 32):
            rows = pl.ds(lo, 32)
            acc = mb[rows]
            for m in range(STEP):
                acc = acc + z[at + m, rows] * cs[m : m + 1]
            mb[rows] = acc
        return carry

    lax.fori_loop(0, kb // STEP, body, 0, unroll=2)
    b_rows, c_rows, a_gram = b[...], c[...], ata[...]
    b_gram, c_gram = gram(b_rows), gram(c_rows)
    bc_gram[...] = b_gram * c_gram
    for_b = mult_b * (mb[...] - apply(b_rows, a_gram * c_gram))
    for_c = mult_c * (mc[...] - apply(c_rows, a_gram * b_gram))
    place(core, for_b, for_c, keep, send)


def shards(tiles, slot, a, b, c, va, vb, vc):
    wide = lax.axis_size("wide")
    narrow = lax.axis_size("narrow")
    chips = narrow // CORES
    core = lax.axis_index("narrow") % CORES
    lead = core == 0
    ib, jb, kb = a.shape[0], b.shape[0], c.shape[0]
    rank = a.shape[1]
    half = jb // CORES
    scale_a = 1.0 / (jb * kb)
    mults = dict(
        mult_b=step_rate / (narrow * ib * kb), mult_c=step_rate / (narrow * ib * jb)
    )
    far = in_hbm(tiles)
    core_arg = core.astype(jnp.int32).reshape(1)

    def permute(x, where):
        route = []
        for w in range(wide):
            for n in range(narrow):
                to = where(n // CORES, n % CORES)
                if to is not None:
                    ahead, chip, unit = to
                    target = (w + ahead) % wide * narrow + chip % chips * CORES + unit % CORES
                    route.append((w * narrow + n, target))
        return lax.ppermute(x, BOTH, route)

    def swap(x):
        return permute(x, lambda y, u: (0, y, u + 1))

    turns = range(chips)
    thirds = [[t for t in turns if t % CORES == u] for u in range(CORES)]
    plan = [
        [("b", t) for t in turns] + [("c", t) for t in thirds[0]],
        [("c", t) for t in thirds[1]] + [("b", t) for t in turns],
    ]
    length = max(map(len, plan))
    plan = [p + [None] * (length - len(p)) for p in plan]

    def onward(total):
        part = {"b": total[:half], "c": total[half:]}
        ahead = {"b": SECOND_STRIDE, "c": THIRD_STRIDE}
        got = []
        for pair in zip(*plan, strict=True):
            kinds = [p and p[0] for p in pair]

            def where(y, u, pair=pair):
                return pair[u] and (ahead[pair[u][0]], y + pair[u][1], u)

            if kinds[0] == kinds[1] or None in kinds:
                message = part[kinds[0] or kinds[1]]
            else:
                message = jnp.where(lead, part[kinds[0]], part[kinds[1]])
            got.append(permute(message, where))
        return got

    def collect(got, kind):
        sums = []
        for u in range(CORES):
            terms = [x for x, pair in zip(got, zip(*plan)) if pair[u] and pair[u][0] == kind]
            sums.append(functools.reduce(jnp.add, terms) if terms else jnp.zeros_like(got[0]))
        return jnp.where(lead, sums[0], sums[1])

    def around(x):
        return [permute(x, lambda y, u, t=t: (0, y + t, u)) for t in range(1, chips)]

    def ordered(mine, other):
        return jnp.where(lead, jnp.concatenate([mine, other], axis=0), jnp.concatenate([other, mine], axis=0))

    tile_shape = jax.ShapeDtypeStruct((kb, ib, jb), tiles.dtype)
    block_a, block_b, block_c, share = f32(ib, rank), f32(jb, rank), f32(kb, rank), f32(half + kb, rank)

    grams = f32(rank, rank)

    def scratch(x):
        return pltpu.VMEM(x.shape, x.dtype)

    args = a, b, c, va, vb, vc
    tile, a, b, c, va, bc_gram, keep, send = pl.pallas_call(
        functools.partial(first_kernel, chips=chips, **mults),
        out_shape=(tile_shape, block_a, block_b, block_c, block_a, grams, share, share),
        in_specs=[SMEM, SMEM] + [HBM] * 7,
        out_specs=(VMEM,) * 8,
        scratch_shapes=[scratch(x) for x in (block_b, block_c, block_b, block_c)]
        + [pltpu.SemaphoreType.DMA((4,)), pltpu.SemaphoreType.DMA((6,))],
        compiler_params=GRANT,
    )(core_arg, slot, far, *map(in_hbm, args))
    now = jnp.where(lead, b, jnp.pad(c, ((0, jb - kb), (0, 0))))
    for s in range(STRATA):
        received = swap(send)
        total = keep + received
        total, now, tile, a, va, b, c, bc_gram = lax.optimization_barrier(
            (total, now, tile, a, va, b, c, bc_gram)
        )
        if s + 1 == STRATA:
            break
        got = onward(total)
        past = permute(now, lambda y, u: ((SECOND_STRIDE, THIRD_STRIDE)[u], y, u))
        tile, a, va, ata, z = pl.pallas_call(
            functools.partial(window_kernel, scale=scale_a, stratum=s + 1),
            out_shape=(tile_shape, block_a, block_a, grams, f32(kb, jb, rank)),
            in_specs=[SMEM, HBM] + [VMEM] * 6,
            out_specs=(VMEM,) * 5,
            scratch_shapes=[pltpu.SemaphoreType.DMA],
            compiler_params=GRANT,
        )(slot, far, tile, a, va, b, c, bc_gram)
        got, a, va, ata, z = lax.optimization_barrier((got, a, va, ata, z))
        mine = jnp.concatenate([collect(got, "b"), collect(got, "c")], axis=0)
        other = swap(mine)
        b, c, now, bc_gram, keep, send = pl.pallas_call(
            functools.partial(gradient_kernel, **mults),
            out_shape=(block_b, block_c, block_b, grams, share, share),
            in_specs=[SMEM] + [VMEM] * 6,
            out_specs=(VMEM,) * 6,
            scratch_shapes=[scratch(block_b), scratch(block_c)],
            compiler_params=GRANT,
        )(core_arg, tile, z, a, ata, mine, other)
        base = ((1.0 + momentum) * now - momentum * past) * (1.0 / chips)
        none = jnp.zeros((half, rank), jnp.float32)
        for_c = jnp.where(lead, 0.0, base[:kb])
        keep = keep + jnp.concatenate([jnp.where(lead, base[:half], none), for_c], axis=0)
        send = send + jnp.concatenate([jnp.where(lead, base[half:], none), for_c], axis=0)
    others = around(total)
    a = pl.pallas_call(
        functools.partial(last_kernel, scale=scale_a),
        out_shape=f32(ib, rank),
        in_specs=[VMEM] * 6,
        out_specs=VMEM,
        compiler_params=GRANT,
    )(tile, a, va, b, c, bc_gram)
    others, a = lax.optimization_barrier((others, a))
    total = functools.reduce(jnp.add, others, total)
    return a, ordered(total[:half], swap(total[:half])), total[half:]


def solution(mesh):
    return program(mesh)


def program(mesh):
    return jax.shard_map(
        shards,
        mesh=mesh,
        in_specs=(
            P(None, None, BOTH, None),
            P(BOTH, None),
            P(BOTH, None),
            P("wide", None),
            P("wide", None),
            P(BOTH, None),
            P("wide", None),
            P("wide", None),
        ),
        out_specs=(P(BOTH, None), P("wide", None), P("wide", None)),
        check_vma=False,
    )
```

profile of v0, /device:TPU:0, one launch (start us, length us, event | category | flops | bytes accessed | tf_op | source)
XLA Modules:
  0.0 80.6 jit_solution(14944895413046678053)
XLA Ops:
  0.6 0.0 copy-start
  0.7 0.6 copy-done
  1.3 5.4 %shard_map.103 = (bf16[64,64,128]{2,1,0:T(8,128)(2,1)S(1)}, f32[64,256]{1,0:T(8,128)S(1)}, f32[128,256]{1,0:T(8,128)S(1)}, f32[64,256]{1,0:T(8,128)S(1)}, f32[64...) custom-call(s32[1]{0:T(128)} %bitcast.core, s32[1,4]{1,0:T(1,128)S(1)} %copy-done, ...), custom_call_target="tpu_custom_call" | custom-call | tf_op jit(solution)/shard_map/pallas_call | solution.py:324
  6.7 0.6 collective-permute-start
  7.3 1.0 %collective-permute-done = f32[128,256]{1,0:T(8,128)S(1)} collective-permute-done((f32[128,256]{1,0:T(8,128)S(1)}, f32[128,256]{1,0:T(8,128)S(1)}, u32[]{:S(2)}, u32[]{:S(2)}) %collective-permute-start) | collective-permute-done | bytes 131104 | tf_op jit(solution)/shard_map/ppermute | solution.py:271
  8.3 2.9 %collective-permute-start.1 = (f32[64,256]{1,0:T(8,128)S(1)}, f32[64,256]{1,0:T(8,128)S(1)}, u32[]{:S(2)}, u32[]{:S(2)}) collective-permute-start(f32[64,256]{1,0:T(8,128)S(1)} %get-tuple-element.217), channel_id=1, source_target_pairs={{0,4},{1,15},{2,6},{3,13},{4,8},{5,19},{6,10},{7,17},{8,12},{9,23}... | collective-permute-start | bytes 196616 | tf_op jit(solution)/shard_map/ppermute | solution.py:271
  11.2 2.5 %collective-permute-start.2 = (f32[64,256]{1,0:T(8,128)S(1)}, f32[64,256]{1,0:T(8,128)S(1)}, u32[]{:S(2)}, u32[]{:S(2)}) collective-permute-start(f32[64,256]{1,0:T(8,128)S(1)} %get-tuple-element.218), channel_id=1, source_target_pairs={{0,6},{1,5},{2,4},{3,7},{4,10},{5,9},{6,8},{7,11},{8,14},{9,13},{1... | collective-permute-start | bytes 196616 | tf_op jit(solution)/shard_map/ppermute | solution.py:271
  13.7 2.5 %collective-permute-start.3 = (f32[64,256]{1,0:T(8,128)S(1)}, f32[64,256]{1,0:T(8,128)S(1)}, u32[]{:S(2)}, u32[]{:S(2)}) collective-permute-start(f32[64,256]{1,0:T(8,128)S(1)} %get-tuple-element.216), channel_id=1, source_target_pairs={{0,12},{1,7},{2,14},{3,5},{4,16},{5,11},{6,18},{7,9},{8,20},{9,15}... | collective-permute-start | bytes 196616 | tf_op jit(solution)/shard_map/ppermute | solution.py:271
  16.2 0.0 copy-start.1
  16.2 0.7 copy-done.1
  16.9 4.2 %shard_map.104 = (bf16[64,64,128]{2,1,0:T(8,128)(2,1)S(1)}, f32[64,256]{1,0:T(8,128)S(1)}, f32[64,256]{1,0:T(8,128)S(1)}, f32[256,256]{1,0:T(8,128)S(1)}, f32[64,128,256]{2,1,0:T(8,128)S(1)}) custom-call(s32[1,4]{1,0:T(1,128)S(1)} %copy-done.1, bf16[4,64,64,128]{3,2,1,0:T(8,128)(2,1)} %tiles.7, bf16[64,64,128]{2,1,0:T(8,128)(2,1)S(1)} %get-tuple-element.106.old, ...), custom_call_target="tpu_custom_call" | custom-call | tf_op jit(solution)/shard_map/pallas_call | solution.py:344
  21.1 0.0 collective-permute-done.1
  21.1 0.0 collective-permute-done.2
  21.1 0.8 collective-permute-done.3
  21.9 0.1 collective-permute-start.4
  22.0 0.8 %collective-permute-start.5 = (f32[128,256]{1,0:T(8,128)S(1)}, f32[128,256]{1,0:T(8,128)S(1)}, u32[]{:S(2)}, u32[]{:S(2)}) collective-permute-start(f32[128,256]{1,0:T(8,128)S(1)} %pad_select_fusion), channel_id=1, source_target_pairs={{0,4},{1,13},{2,6},{3,15},{4,8},{5,17},{6,10},{7,19},{8,12},{9,21}... | collective-permute-start | bytes 393224 | tf_op jit(solution)/shard_map/ppermute | solution.py:271
  22.8 0.5 collective-permute-done.4.other
  23.3 2.3 %shard_map.105 = (f32[128,256]{1,0:T(8,128)S(1)}, f32[64,256]{1,0:T(8,128)S(1)}, f32[128,256]{1,0:T(8,128)S(1)}, f32[256,256]{1,0:T(8,128)S(1)}, f32[128,256]{1,0:T(8,128)S(1)}, /*index=5*/f32[128,256]{1,0:T(8,128)S(1)}) custom-call(s32[1]{0:T(128)} %bitcast.core, bf16[64,64,128]{2,1,0:T(8,128)(2,1)S(1)} %get-tuple-element.132.tile.old, ...), custom_call_target="tpu_custom_call" | custom-call | tf_op jit(solution)/shard_map/pallas_call | solution.py:355
  25.6 4.4 %collective-permute-done.5 = f32[128,256]{1,0:T(8,128)S(1)} collective-permute-done((f32[128,256]{1,0:T(8,128)S(1)}, f32[128,256]{1,0:T(8,128)S(1)}, u32[]{:S(2)}, u32[]{:S(2)}) %collective-permute-start.5) | collective-permute-done | bytes 131104 | tf_op jit(solution)/shard_map/ppermute | solution.py:271
  30.1 0.9 %collective-permute-start.6 = (f32[128,256]{1,0:T(8,128)S(1)}, f32[128,256]{1,0:T(8,128)S(1)}, u32[]{:S(2)}, u32[]{:S(2)}) collective-permute-start(f32[128,256]{1,0:T(8,128)S(1)} %fusion.8), channel_id=1, source_target_pairs={{0,1},{1,0},{2,3},{3,2},{4,5},{5,4},{6,7},{7,6},{8,9},{9,8},{10,11... | collective-permute-start | bytes 393224 | tf_op jit(solution)/shard_map/ppermute | solution.py:271
  31.0 1.0 %collective-permute-done.6 = f32[128,256]{1,0:T(8,128)S(1)} collective-permute-done((f32[128,256]{1,0:T(8,128)S(1)}, f32[128,256]{1,0:T(8,128)S(1)}, u32[]{:S(2)}, u32[]{:S(2)}) %collective-permute-start.6) | collective-permute-done | bytes 131104 | tf_op jit(solution)/shard_map/ppermute | solution.py:271
  32.1 0.1 collective-permute-start.7
  32.1 1.3 %collective-permute-start.8 = (f32[64,256]{1,0:T(8,128)S(1)}, f32[64,256]{1,0:T(8,128)S(1)}, u32[]{:S(2)}, u32[]{:S(2)}) collective-permute-start(f32[64,256]{1,0:T(8,128)S(1)} %get-tuple-element.210), channel_id=1, source_target_pairs={{0,6},{1,5},{2,4},{3,7},{4,10},{5,9},{6,8},{7,11},{8,14},{9,13},{1... | collective-permute-start | bytes 196616 | tf_op jit(solution)/shard_map/ppermute | solution.py:271
  33.4 1.9 %collective-permute-start.9 = (f32[64,256]{1,0:T(8,128)S(1)}, f32[64,256]{1,0:T(8,128)S(1)}, u32[]{:S(2)}, u32[]{:S(2)}) collective-permute-start(f32[64,256]{1,0:T(8,128)S(1)} %get-tuple-element.208), channel_id=1, source_target_pairs={{0,12},{1,7},{2,14},{3,5},{4,16},{5,11},{6,18},{7,9},{8,20},{9,15}... | collective-permute-start | bytes 196616 | tf_op jit(solution)/shard_map/ppermute | solution.py:271
  35.3 4.2 %shard_map.106 = (bf16[64,64,128]{2,1,0:T(8,128)(2,1)S(1)}, f32[64,256]{1,0:T(8,128)S(1)}, f32[64,256]{1,0:T(8,128)S(1)}, f32[256,256]{1,0:T(8,128)S(1)}, f32[64,128,256]{2,1,0:T(8,128)S(1)}) custom-call(s32[1,4]{1,0:T(1,128)S(1)} %copy-done.1, bf16[4,64,64,128]{3,2,1,0:T(8,128)(2,1)} %tiles.7, bf16[64,64,128]{2,1,0:T(8,128)(2,1)S(1)} %get-tuple-element.132.tile.old, ...), custom_call_target="tpu_custom_call" | custom-call | tf_op jit(solution)/shard_map/pallas_call | solution.py:344
  39.5 0.0 collective-permute-done.7
  39.5 0.6 collective-permute-done.8
  40.0 0.6 collective-permute-done.9
  40.7 1.5 %collective-permute-start.10 = (f32[128,256]{1,0:T(8,128)S(1)}, f32[128,256]{1,0:T(8,128)S(1)}, u32[]{:S(2)}, u32[]{:S(2)}) collective-permute-start(f32[128,256]{1,0:T(8,128)S(1)} %pad_maximum_fusion.7.mine), channel_id=1, source_target_pairs={{0,1},{1,0},{2,3},{3,2},{4,5},{5,4},{6,7},{7,6},{8,9},{9,8},{10,11... | collective-permute-start | bytes 393224 | tf_op jit(solution)/shard_map/ppermute | solution.py:271
  42.2 0.0 collective-permute-start.11
  42.2 1.0 %collective-permute-done.10.other = f32[128,256]{1,0:T(8,128)S(1)} collective-permute-done((f32[128,256]{1,0:T(8,128)S(1)}, f32[128,256]{1,0:T(8,128)S(1)}, u32[]{:S(2)}, u32[]{:S(2)}) %collective-permute-start.10) | collective-permute-done | bytes 131104 | tf_op jit(solution)/shard_map/ppermute | solution.py:271
  43.2 2.3 %shard_map.107 = (f32[128,256]{1,0:T(8,128)S(1)}, f32[64,256]{1,0:T(8,128)S(1)}, f32[128,256]{1,0:T(8,128)S(1)}, f32[256,256]{1,0:T(8,128)S(1)}, f32[128,256]{1,0:T(8,128)S(1)}, /*index=5*/f32[128,256]{1,0:T(8,128)S(1)}) custom-call(s32[1]{0:T(128)} %bitcast.core, bf16[64,64,128]{2,1,0:T(8,128)(2,1)S(1)} %get-tuple-element.158.tile.old, ...), custom_call_target="tpu_custom_call" | custom-call | tf_op jit(solution)/shard_map/pallas_call | solution.py:355
  45.5 4.4 %collective-permute-done.11 = f32[128,256]{1,0:T(8,128)S(1)} collective-permute-done((f32[128,256]{1,0:T(8,128)S(1)}, f32[128,256]{1,0:T(8,128)S(1)}, u32[]{:S(2)}, u32[]{:S(2)}) %collective-permute-start.11) | collective-permute-done | bytes 131104 | tf_op jit(solution)/shard_map/ppermute | solution.py:271
  50.0 0.8 %collective-permute-start.12 = (f32[128,256]{1,0:T(8,128)S(1)}, f32[128,256]{1,0:T(8,128)S(1)}, u32[]{:S(2)}, u32[]{:S(2)}) collective-permute-start(f32[128,256]{1,0:T(8,128)S(1)} %fusion.5), channel_id=1, source_target_pairs={{0,1},{1,0},{2,3},{3,2},{4,5},{5,4},{6,7},{7,6},{8,9},{9,8},{10,11... | collective-permute-start | bytes 393224 | tf_op jit(solution)/shard_map/ppermute | solution.py:271
  50.8 1.0 %collective-permute-done.12 = f32[128,256]{1,0:T(8,128)S(1)} collective-permute-done((f32[128,256]{1,0:T(8,128)S(1)}, f32[128,256]{1,0:T(8,128)S(1)}, u32[]{:S(2)}, u32[]{:S(2)}) %collective-permute-start.12) | collective-permute-done | bytes 131104 | tf_op jit(solution)/shard_map/ppermute | solution.py:271
  51.9 0.1 collective-permute-start.13
  51.9 1.8 %collective-permute-start.14 = (f32[64,256]{1,0:T(8,128)S(1)}, f32[64,256]{1,0:T(8,128)S(1)}, u32[]{:S(2)}, u32[]{:S(2)}) collective-permute-start(f32[64,256]{1,0:T(8,128)S(1)} %get-tuple-element.202), channel_id=1, source_target_pairs={{0,6},{1,5},{2,4},{3,7},{4,10},{5,9},{6,8},{7,11},{8,14},{9,13},{1... | collective-permute-start | bytes 196616 | tf_op jit(solution)/shard_map/ppermute | solution.py:271
  53.7 2.3 %collective-permute-start.15 = (f32[64,256]{1,0:T(8,128)S(1)}, f32[64,256]{1,0:T(8,128)S(1)}, u32[]{:S(2)}, u32[]{:S(2)}) collective-permute-start(f32[64,256]{1,0:T(8,128)S(1)} %get-tuple-element.200), channel_id=1, source_target_pairs={{0,12},{1,7},{2,14},{3,5},{4,16},{5,11},{6,18},{7,9},{8,20},{9,15}... | collective-permute-start | bytes 196616 | tf_op jit(solution)/shard_map/ppermute | solution.py:271
  56.0 4.2 %shard_map.108 = (bf16[64,64,128]{2,1,0:T(8,128)(2,1)S(1)}, f32[64,256]{1,0:T(8,128)S(1)}, f32[64,256]{1,0:T(8,128)S(1)}, f32[256,256]{1,0:T(8,128)S(1)}, f32[64,128,256]{2,1,0:T(8,128)S(1)}) custom-call(s32[1,4]{1,0:T(1,128)S(1)} %copy-done.1, bf16[4,64,64,128]{3,2,1,0:T(8,128)(2,1)} %tiles.7, bf16[64,64,128]{2,1,0:T(8,128)(2,1)S(1)} %get-tuple-element.158.tile.old, ...), custom_call_target="tpu_custom_call" | custom-call | tf_op jit(solution)/shard_map/pallas_call | solution.py:344
  60.2 0.0 collective-permute-done.13
  60.2 0.5 collective-permute-done.14
  60.7 1.7 %collective-permute-done.15 = f32[64,256]{1,0:T(8,128)S(1)} collective-permute-done((f32[64,256]{1,0:T(8,128)S(1)}, f32[64,256]{1,0:T(8,128)S(1)}, u32[]{:S(2)}, u32[]{:S(2)}) %collective-permute-start.15) | collective-permute-done | bytes 65568 | tf_op jit(solution)/shard_map/ppermute | solution.py:271
  62.5 0.1 collective-permute-start.16
  62.6 0.2 collective-permute-start.17
  62.8 1.1 %collective-permute-done.16.other = f32[128,256]{1,0:T(8,128)S(1)} collective-permute-done((f32[128,256]{1,0:T(8,128)S(1)}, f32[128,256]{1,0:T(8,128)S(1)}, u32[]{:S(2)}, u32[]{:S(2)}) %collective-permute-start.16) | collective-permute-done | bytes 131104 | tf_op jit(solution)/shard_map/ppermute | solution.py:271
  63.9 2.3 %shard_map.109 = (f32[128,256]{1,0:T(8,128)S(1)}, f32[64,256]{1,0:T(8,128)S(1)}, f32[128,256]{1,0:T(8,128)S(1)}, f32[256,256]{1,0:T(8,128)S(1)}, f32[128,256]{1,0:T(8,128)S(1)}, /*index=5*/f32[128,256]{1,0:T(8,128)S(1)}) custom-call(s32[1]{0:T(128)} %bitcast.core, bf16[64,64,128]{2,1,0:T(8,128)(2,1)S(1)} %get-tuple-element.185.tile.old, ...), custom_call_target="tpu_custom_call" | custom-call | tf_op jit(solution)/shard_map/pallas_call | solution.py:355
  66.3 4.0 %collective-permute-done.17 = f32[128,256]{1,0:T(8,128)S(1)} collective-permute-done((f32[128,256]{1,0:T(8,128)S(1)}, f32[128,256]{1,0:T(8,128)S(1)}, u32[]{:S(2)}, u32[]{:S(2)}) %collective-permute-start.17) | collective-permute-done | bytes 131104 | tf_op jit(solution)/shard_map/ppermute | solution.py:271
  70.4 0.8 collective-permute-start.18
  71.2 1.0 %collective-permute-done.18 = f32[128,256]{1,0:T(8,128)S(1)} collective-permute-done((f32[128,256]{1,0:T(8,128)S(1)}, f32[128,256]{1,0:T(8,128)S(1)}, u32[]{:S(2)}, u32[]{:S(2)}) %collective-permute-start.18) | collective-permute-done | bytes 131104 | tf_op jit(solution)/shard_map/ppermute | solution.py:271
  72.2 0.7 collective-permute-start.19
  72.9 2.2 %shard_map.110 = f32[64,256]{1,0:T(8,128)} custom-call(bf16[64,64,128]{2,1,0:T(8,128)(2,1)S(1)} %get-tuple-element.185.tile.old, f32[64,256]{1,0:T(8,128)S(1)} %get-tuple-element.186.a, f32[64,256]{1,0:T(8,128)S(1)} %get-tuple-element.187.va, f32[128,256]{1,0:T(8,128)S(1)} %get-tuple-element.188.b, f32[64,256]{1,0:T(8,128)S(1)} %get-tuple-element.189.c, ...), custom_call_target="tpu_custom_call" | custom-call | tf_op jit(solution)/shard_map/pallas_call | solution.py:369
  75.0 3.0 %collective-permute-done.19 = f32[128,256]{1,0:T(8,128)S(1)} collective-permute-done((f32[128,256]{1,0:T(8,128)S(1)}, f32[128,256]{1,0:T(8,128)S(1)}, u32[]{:S(2)}, u32[]{:S(2)}) %collective-permute-start.19) | collective-permute-done | bytes 131104 | tf_op jit(solution)/shard_map/ppermute | solution.py:271
  78.1 0.6 fusion.9
  78.7 0.0 collective-permute-start.20
  78.7 1.3 %collective-permute-done.20 = f32[64,256]{1,0:T(8,128)S(1)} collective-permute-done((f32[64,256]{1,0:T(8,128)S(1)}, f32[64,256]{1,0:T(8,128)S(1)}, u32[]{:S(2)}, u32[]{:S(2)}) %collective-permute-start.20) | collective-permute-done | bytes 65568 | tf_op jit(solution)/shard_map/ppermute | solution.py:271
  79.9 0.7 maximum_select_fusion
  (24 shorter events, 0.4 us)
Async XLA Ops:
  0.6 0.7 copy-start
  6.7 1.5 %collective-permute-start = (f32[128,256]{1,0:T(8,128)S(1)}, f32[128,256]{1,0:T(8,128)S(1)}, u32[]{:S(2)}, u32[]{:S(2)}) collective-permute-start(f32[128,256]{1,0:T(8,128)S(1)} %get-tuple-element.99), channel_id=1, source_target_pairs={{0,1},{1,0},{2,3},{3,2},{4,5},{5,4},{6,7},{7,6},{8,9},{9,8},{10,11... | collective-permute-start | bytes 393224 | tf_op jit(solution)/shard_map/ppermute | solution.py:271
  8.3 12.7 %collective-permute-start.1 = (f32[64,256]{1,0:T(8,128)S(1)}, f32[64,256]{1,0:T(8,128)S(1)}, u32[]{:S(2)}, u32[]{:S(2)}) collective-permute-start(f32[64,256]{1,0:T(8,128)S(1)} %get-tuple-element.217), channel_id=1, source_target_pairs={{0,4},{1,15},{2,6},{3,13},{4,8},{5,19},{6,10},{7,17},{8,12},{9,23}... | collective-permute-start | bytes 196616 | tf_op jit(solution)/shard_map/ppermute | solution.py:271
  11.2 9.9 %collective-permute-start.2 = (f32[64,256]{1,0:T(8,128)S(1)}, f32[64,256]{1,0:T(8,128)S(1)}, u32[]{:S(2)}, u32[]{:S(2)}) collective-permute-start(f32[64,256]{1,0:T(8,128)S(1)} %get-tuple-element.218), channel_id=1, source_target_pairs={{0,6},{1,5},{2,4},{3,7},{4,10},{5,9},{6,8},{7,11},{8,14},{9,13},{1... | collective-permute-start | bytes 196616 | tf_op jit(solution)/shard_map/ppermute | solution.py:271
  13.7 8.1 %collective-permute-start.3 = (f32[64,256]{1,0:T(8,128)S(1)}, f32[64,256]{1,0:T(8,128)S(1)}, u32[]{:S(2)}, u32[]{:S(2)}) collective-permute-start(f32[64,256]{1,0:T(8,128)S(1)} %get-tuple-element.216), channel_id=1, source_target_pairs={{0,12},{1,7},{2,14},{3,5},{4,16},{5,11},{6,18},{7,9},{8,20},{9,15}... | collective-permute-start | bytes 196616 | tf_op jit(solution)/shard_map/ppermute | solution.py:271
  16.2 0.7 copy-start.1
  21.9 1.4 %collective-permute-start.4 = (f32[128,256]{1,0:T(8,128)S(1)}, f32[128,256]{1,0:T(8,128)S(1)}, u32[]{:S(2)}, u32[]{:S(2)}) collective-permute-start(f32[128,256]{1,0:T(8,128)S(1)} %pad_maximum_fusion.6.mine), channel_id=1, source_target_pairs={{0,1},{1,0},{2,3},{3,2},{4,5},{5,4},{6,7},{7,6},{8,9},{9,8},{10,11... | collective-permute-start | bytes 393224 | tf_op jit(solution)/shard_map/ppermute | solution.py:271
  22.0 8.1 %collective-permute-start.5 = (f32[128,256]{1,0:T(8,128)S(1)}, f32[128,256]{1,0:T(8,128)S(1)}, u32[]{:S(2)}, u32[]{:S(2)}) collective-permute-start(f32[128,256]{1,0:T(8,128)S(1)} %pad_select_fusion), channel_id=1, source_target_pairs={{0,4},{1,13},{2,6},{3,15},{4,8},{5,17},{6,10},{7,19},{8,12},{9,21}... | collective-permute-start | bytes 393224 | tf_op jit(solution)/shard_map/ppermute | solution.py:271
  30.1 1.9 %collective-permute-start.6 = (f32[128,256]{1,0:T(8,128)S(1)}, f32[128,256]{1,0:T(8,128)S(1)}, u32[]{:S(2)}, u32[]{:S(2)}) collective-permute-start(f32[128,256]{1,0:T(8,128)S(1)} %fusion.8), channel_id=1, source_target_pairs={{0,1},{1,0},{2,3},{3,2},{4,5},{5,4},{6,7},{7,6},{8,9},{9,8},{10,11... | collective-permute-start | bytes 393224 | tf_op jit(solution)/shard_map/ppermute | solution.py:271
  32.1 7.4 %collective-permute-start.7 = (f32[64,256]{1,0:T(8,128)S(1)}, f32[64,256]{1,0:T(8,128)S(1)}, u32[]{:S(2)}, u32[]{:S(2)}) collective-permute-start(f32[64,256]{1,0:T(8,128)S(1)} %get-tuple-element.209), channel_id=1, source_target_pairs={{0,4},{1,15},{2,6},{3,13},{4,8},{5,19},{6,10},{7,17},{8,12},{9,23}... | collective-permute-start | bytes 196616 | tf_op jit(solution)/shard_map/ppermute | solution.py:271
  32.1 7.9 %collective-permute-start.8 = (f32[64,256]{1,0:T(8,128)S(1)}, f32[64,256]{1,0:T(8,128)S(1)}, u32[]{:S(2)}, u32[]{:S(2)}) collective-permute-start(f32[64,256]{1,0:T(8,128)S(1)} %get-tuple-element.210), channel_id=1, source_target_pairs={{0,6},{1,5},{2,4},{3,7},{4,10},{5,9},{6,8},{7,11},{8,14},{9,13},{1... | collective-permute-start | bytes 196616 | tf_op jit(solution)/shard_map/ppermute | solution.py:271
  33.4 7.2 %collective-permute-start.9 = (f32[64,256]{1,0:T(8,128)S(1)}, f32[64,256]{1,0:T(8,128)S(1)}, u32[]{:S(2)}, u32[]{:S(2)}) collective-permute-start(f32[64,256]{1,0:T(8,128)S(1)} %get-tuple-element.208), channel_id=1, source_target_pairs={{0,12},{1,7},{2,14},{3,5},{4,16},{5,11},{6,18},{7,9},{8,20},{9,15}... | collective-permute-start | bytes 196616 | tf_op jit(solution)/shard_map/ppermute | solution.py:271
  40.7 2.5 %collective-permute-start.10 = (f32[128,256]{1,0:T(8,128)S(1)}, f32[128,256]{1,0:T(8,128)S(1)}, u32[]{:S(2)}, u32[]{:S(2)}) collective-permute-start(f32[128,256]{1,0:T(8,128)S(1)} %pad_maximum_fusion.7.mine), channel_id=1, source_target_pairs={{0,1},{1,0},{2,3},{3,2},{4,5},{5,4},{6,7},{7,6},{8,9},{9,8},{10,11... | collective-permute-start | bytes 393224 | tf_op jit(solution)/shard_map/ppermute | solution.py:271
  42.2 7.7 %collective-permute-start.11 = (f32[128,256]{1,0:T(8,128)S(1)}, f32[128,256]{1,0:T(8,128)S(1)}, u32[]{:S(2)}, u32[]{:S(2)}) collective-permute-start(f32[128,256]{1,0:T(8,128)S(1)} %get-tuple-element.152), channel_id=1, source_target_pairs={{0,4},{1,13},{2,6},{3,15},{4,8},{5,17},{6,10},{7,19},{8,12},{9,21}... | collective-permute-start | bytes 393224 | tf_op jit(solution)/shard_map/ppermute | solution.py:271
  50.0 1.8 %collective-permute-start.12 = (f32[128,256]{1,0:T(8,128)S(1)}, f32[128,256]{1,0:T(8,128)S(1)}, u32[]{:S(2)}, u32[]{:S(2)}) collective-permute-start(f32[128,256]{1,0:T(8,128)S(1)} %fusion.5), channel_id=1, source_target_pairs={{0,1},{1,0},{2,3},{3,2},{4,5},{5,4},{6,7},{7,6},{8,9},{9,8},{10,11... | collective-permute-start | bytes 393224 | tf_op jit(solution)/shard_map/ppermute | solution.py:271
  51.9 8.3 %collective-permute-start.13 = (f32[64,256]{1,0:T(8,128)S(1)}, f32[64,256]{1,0:T(8,128)S(1)}, u32[]{:S(2)}, u32[]{:S(2)}) collective-permute-start(f32[64,256]{1,0:T(8,128)S(1)} %get-tuple-element.201), channel_id=1, source_target_pairs={{0,4},{1,15},{2,6},{3,13},{4,8},{5,19},{6,10},{7,17},{8,12},{9,23}... | collective-permute-start | bytes 196616 | tf_op jit(solution)/shard_map/ppermute | solution.py:271
  51.9 8.8 %collective-permute-start.14 = (f32[64,256]{1,0:T(8,128)S(1)}, f32[64,256]{1,0:T(8,128)S(1)}, u32[]{:S(2)}, u32[]{:S(2)}) collective-permute-start(f32[64,256]{1,0:T(8,128)S(1)} %get-tuple-element.202), channel_id=1, source_target_pairs={{0,6},{1,5},{2,4},{3,7},{4,10},{5,9},{6,8},{7,11},{8,14},{9,13},{1... | collective-permute-start | bytes 196616 | tf_op jit(solution)/shard_map/ppermute | solution.py:271
  53.7 8.7 %collective-permute-start.15 = (f32[64,256]{1,0:T(8,128)S(1)}, f32[64,256]{1,0:T(8,128)S(1)}, u32[]{:S(2)}, u32[]{:S(2)}) collective-permute-start(f32[64,256]{1,0:T(8,128)S(1)} %get-tuple-element.200), channel_id=1, source_target_pairs={{0,12},{1,7},{2,14},{3,5},{4,16},{5,11},{6,18},{7,9},{8,20},{9,15}... | collective-permute-start | bytes 196616 | tf_op jit(solution)/shard_map/ppermute | solution.py:271
  62.5 1.4 %collective-permute-start.16 = (f32[128,256]{1,0:T(8,128)S(1)}, f32[128,256]{1,0:T(8,128)S(1)}, u32[]{:S(2)}, u32[]{:S(2)}) collective-permute-start(f32[128,256]{1,0:T(8,128)S(1)} %pad_maximum_fusion.8.mine), channel_id=1, source_target_pairs={{0,1},{1,0},{2,3},{3,2},{4,5},{5,4},{6,7},{7,6},{8,9},{9,8},{10,11... | collective-permute-start | bytes 393224 | tf_op jit(solution)/shard_map/ppermute | solution.py:271
  62.6 7.7 %collective-permute-start.17 = (f32[128,256]{1,0:T(8,128)S(1)}, f32[128,256]{1,0:T(8,128)S(1)}, u32[]{:S(2)}, u32[]{:S(2)}) collective-permute-start(f32[128,256]{1,0:T(8,128)S(1)} %get-tuple-element.178), channel_id=1, source_target_pairs={{0,4},{1,13},{2,6},{3,15},{4,8},{5,17},{6,10},{7,19},{8,12},{9,21}... | collective-permute-start | bytes 393224 | tf_op jit(solution)/shard_map/ppermute | solution.py:271
  70.4 1.8 %collective-permute-start.18 = (f32[128,256]{1,0:T(8,128)S(1)}, f32[128,256]{1,0:T(8,128)S(1)}, u32[]{:S(2)}, u32[]{:S(2)}) collective-permute-start(f32[128,256]{1,0:T(8,128)S(1)} %fusion.2), channel_id=1, source_target_pairs={{0,1},{1,0},{2,3},{3,2},{4,5},{5,4},{6,7},{7,6},{8,9},{9,8},{10,11... | collective-permute-start | bytes 393224 | tf_op jit(solution)/shard_map/ppermute | solution.py:271
  72.2 5.8 %collective-permute-start.19 = (f32[128,256]{1,0:T(8,128)S(1)}, f32[128,256]{1,0:T(8,128)S(1)}, u32[]{:S(2)}, u32[]{:S(2)}) collective-permute-start(f32[128,256]{1,0:T(8,128)S(1)} %fusion.1), channel_id=1, source_target_pairs={{0,2},{1,3},{2,0},{3,1},{4,6},{5,7},{6,4},{7,5},{8,10},{9,11},{10,... | collective-permute-start | bytes 393224 | tf_op jit(solution)/shard_map/ppermute | solution.py:271
  78.7 1.3 %collective-permute-start.20 = (f32[64,256]{1,0:T(8,128)S(1)}, f32[64,256]{1,0:T(8,128)S(1)}, u32[]{:S(2)}, u32[]{:S(2)}) collective-permute-start(f32[64,256]{1,0:T(8,128)S(1)} %get-tuple-element.194), channel_id=1, source_target_pairs={{0,1},{1,0},{2,3},{3,2},{4,5},{5,4},{6,7},{7,6},{8,9},{9,8},{10,11... | collective-permute-start | bytes 196616 | tf_op jit(solution)/shard_map/ppermute | solution.py:271
where the time goes:
time: 80.8 us; the launch traced here: 80.6 us
  waiting for transfers between devices  27.8 us (34%)
  Pallas kernels  27.1 us (34%)
  starting transfers between devices  21.7 us (27%)
  local copies, waits for them, and re-layouts  1.94 us (2%)
  other arithmetic  1.1 us (1%)
  between operations  0.92 us (1%)
    ppermute x21, waiting for transfers between devices, permute(): return lax.ppermute(x, BOTH, route)  27.8 us
    ppermute x21, starting transfers between devices, permute(): return lax.ppermute(x, BOTH, route)  21.7 us
    pallas_call x3, Pallas kernels, shards(): pl.pallas_call(functools.partial(window_kernel, scale=scale_a, stratum=s...  12.5 us
    pallas_call x3, Pallas kernels, shards(): pl.pallas_call(functools.partial(gradient_kernel, **mults), out_shape=(bl...  7 us
    pallas_call x1, Pallas kernels, shards(): pl.pallas_call(functools.partial(first_kernel, chips=chips, **mults), out...  5.42 us
    pallas_call x1, Pallas kernels, shards(): pl.pallas_call(functools.partial(last_kernel, scale=scale_a), out_shape=f...  2.16 us
  transfers between devices with their start and end apart: 21, of which 17 were waited for; matrix products, arithmetic and copies ran while one was open for 0% of the time, Pallas kernels for 27%

commit v1 on v0

--- a/solution.py
+++ b/solution.py
@@ -103,7 +103,12 @@
     return a[...] - step_rate * va_new, va_new
 
 
-def window_kernel(slot, tiles, old, a, va, b, c, bc_gram, new, a_out, va_out, ata, z, sem, *, scale, stratum):
+def window_kernel(
+    slot_in, tiles, old, a, va, b, c, bc_gram, new, a_out, va_out, ata, z, slot, slot_sem, sem, *, scale, stratum
+):
+    order = pltpu.make_async_copy(slot_in, slot, slot_sem)
+    order.start()
+    order.wait()
     copy = pltpu.make_async_copy(tiles.at[slot[0, stratum]], new, sem)
     copy.start()
     a_new, va_new = advance_a(old, a, va, b, c, bc_gram, scale)
@@ -143,17 +148,19 @@
 
 
 def first_kernel(
-    core, slot, tiles, a_in, b_in, c_in, va_in, vb_in, vc_in, tile, a, b, c, va, bc_gram, keep, send,
-    vb, vc, mb, mc, tile_sem, sem, *, mult_b, mult_c, chips,
+    core, chip, slot_in, tiles, a_in, b_in, c_in, va_in, vb_in, vc_in, tile, a, b, c, va, bc_gram, now, base, keep, send,
+    vb, vc, mb, mc, acc, z, slot, tile_sem, sem, *, mult_b, mult_c,
 ):
     kb, _, jb = tile.shape
     rank = a.shape[1]
     chunks = tile_sem.shape[0]
     size = kb // chunks
     pairs = [(a_in, a), (b_in, b), (c_in, c), (va_in, va), (vb_in, vb), (vc_in, vc)]
+    pairs = [(slot_in, slot)] + pairs
     rest = [pltpu.make_async_copy(x, y, sem.at[n]) for n, (x, y) in enumerate(pairs)]
     for copy in rest:
         copy.start()
+    rest[0].wait()
     source = tiles.at[slot[0, 0]]
     parts = [
         pltpu.make_async_copy(source.at[pl.ds(n * size, size)], tile.at[pl.ds(n * size, size)], tile_sem.at[n])
@@ -161,37 +168,65 @@
     ]
     for copy in parts:
         copy.start()
-    for copy in rest:
+    for copy in rest[1:]:
         copy.wait()
     a_gram = gram(a[...])
-    drag = momentum * step_rate
-    lead = jnp.where(core[0] == 0, 1.0 / chips, 0.0)
     b_gram, c_gram = gram(b[...]), gram(c[...])
     bc_gram[...] = b_gram * c_gram
-    mb[...] = lead * (b[...] - drag * vb[...]) - mult_b * apply(b[...], a_gram * c_gram)
-    base_c = (1.0 / chips - lead) * (c[...] - drag * vc[...]) - mult_c * apply(c[...], a_gram * b_gram)
+    mb[...] = mult_b * apply(b[...], a_gram * c_gram)
+    less_c = mult_c * apply(c[...], a_gram * b_gram)
+    half = jb // CORES
+    drag = momentum * step_rate
+    for u in range(CORES):
+
+        @pl.when(jnp.logical_and(chip[0] == 0, core[0] == u))
+        def _(own=slice(u * half, (u + 1) * half)):
+            now[...] = b[own]
+            base[...] = b[own] - drag * vb[own]
+
+    @pl.when(chip[0] != 0)
+    def _():
+        now[...] = (1.0 / CORES) * c[...]
+        base[...] = (1.0 / CORES) * (c[...] - drag * vc[...])
+
     weights = pair_weights(a[...])
 
-    def body(n, acc):
+    acc[...] = jnp.zeros((jb, rank), jnp.float32)
+
+    def produce(n, slot_of):
+        for m, zk in enumerate(products(tile, pl.multiple_of(n * STEP, STEP), weights)):
+            z[slot_of, m] = zk
+
+    def consume(n, slot_of):
         at = pl.multiple_of(n * STEP, STEP)
         cs = c[pl.ds(at, STEP), :]
-        rows = []
-        for m, zk in enumerate(products(tile, at, weights)):
-            acc = acc + zk * cs[m : m + 1]
-            rows.append(jnp.sum(zk * b[...], axis=0, keepdims=True))
-        mc[pl.ds(at, STEP), :] = jnp.concatenate(rows, axis=0)
-        return acc
-
-    acc = jnp.zeros((jb, rank), jnp.float32)
-    for n, copy in enumerate(parts):
-        copy.wait()
-        acc = lax.fori_loop(n * size // STEP, (n + 1) * size // STEP, body, acc)
-    place(core, mb[...] + mult_b * acc, base_c + mult_c * mc[...], keep, send)
-
-
-def gradient_kernel(core, tile, z, a, ata, mine, other, b, c, now, bc_gram, keep, send, mb, mc, *, mult_b, mult_c):
+        sums = [jnp.zeros((8, rank), jnp.float32)] * STEP
+        for lo in range(0, jb, 32):
+            rows = pl.ds(lo, 32)
+            own, b_rows = acc[rows], b[rows]
+            for m in range(STEP):
+                zk = z[slot_of, m, rows]
+                own = own + zk * cs[m : m + 1]
+                sums[m] = sums[m] + jnp.sum((zk * b_rows).reshape(4, 8, rank), axis=0)
+            acc[rows] = own
+        mc[pl.ds(at, STEP), :] = jnp.concatenate([jnp.sum(x, axis=0, keepdims=True) for x in sums], axis=0)
+
+    per = size // STEP
+    parts[0].wait()
+    produce(0, 0)
+    for n in range(1, kb // STEP):
+        if n % per == 0:
+            parts[n // per].wait()
+        produce(n, n % 2)
+        consume(n - 1, (n - 1) % 2)
+    consume(kb // STEP - 1, (kb // STEP - 1) % 2)
+    place(core, mult_b * acc[...] - mb[...], mult_c * mc[...] - less_c, keep, send)
+
+
+def gradient_kernel(core, tile, z, a, mine, other, b, c, keep, send, mb, mc, y_even, y_odd, *, mult_b, mult_c):
     kb, jb, rank = z.shape
     half = jb // CORES
+    steps = kb // STEP
     first = core[0] == 0
 
     @pl.when(first)
@@ -205,23 +240,12 @@
         b[half:] = mine[:half]
 
     c[...] = mine[half:] + other[half:]
-
-    @pl.when(first)
-    def _():
-        now[...] = b[...]
-
-    @pl.when(jnp.logical_not(first))
-    def _():
-        now[...] = jnp.zeros(now.shape, jnp.float32)
-        now[:kb] = c[...]
-
     stacked = split_rows(b[...])
     a_rows = a[...]
     mb[...] = jnp.zeros((jb, rank), jnp.float32)
 
-    def body(n, carry):
+    def consume(n, y):
         at = pl.multiple_of(n * STEP, STEP)
-        y = slices_times_b(tile, at, stacked)
         mc[pl.ds(at, STEP), :] = jnp.concatenate(
             [jnp.sum(y[m] * a_rows, axis=0, keepdims=True) for m in range(STEP)], axis=0
         )
@@ -232,22 +256,54 @@
             for m in range(STEP):
                 acc = acc + z[at + m, rows] * cs[m : m + 1]
             mb[rows] = acc
+
+    def body(n, carry):
+        y_odd[...] = slices_times_b(tile, pl.multiple_of((2 * n + 1) * STEP, STEP), stacked)
+        consume(2 * n, y_even)
+        after = jnp.minimum(2 * n + 2, steps - 1)
+        y_even[...] = slices_times_b(tile, pl.multiple_of(after * STEP, STEP), stacked)
+        consume(2 * n + 1, y_odd)
         return carry
 
-    lax.fori_loop(0, kb // STEP, body, 0, unroll=2)
-    b_rows, c_rows, a_gram = b[...], c[...], ata[...]
-    b_gram, c_gram = gram(b_rows), gram(c_rows)
+    y_even[...] = slices_times_b(tile, 0, stacked)
+    lax.fori_loop(0, steps // 2, body, 0)
+    place(core, mult_b * mb[...], mult_c * mc[...], keep, send)
+
+
+def terms_kernel(ata, ata_other, mine, b, c, bc_gram, terms, *, mult_b, mult_c):
+    half = b.shape[0] // CORES
+    c_rows = c[...]
+    a_gram, b_gram, c_gram = ata[...] + ata_other[...], gram(b[...]), gram(c_rows)
     bc_gram[...] = b_gram * c_gram
-    for_b = mult_b * (mb[...] - apply(b_rows, a_gram * c_gram))
-    for_c = mult_c * (mc[...] - apply(c_rows, a_gram * b_gram))
-    place(core, for_b, for_c, keep, send)
+    terms[:half] = mult_b * apply(mine[:half], a_gram * c_gram)
+    terms[half:] = mult_c * apply(c_rows, a_gram * b_gram)
+
+
+def final_kernel(core, total, beside, same, cross, b, c):
+    half = beside.shape[0]
+    whole, other = total[...], beside[...]
+    for n in range(same.shape[0]):
+        whole = whole + same[n]
+        other = other + cross[n]
+    c[...] = whole[half:]
+
+    @pl.when(core[0] == 0)
+    def _():
+        b[:half] = whole[:half]
+        b[half:] = other
+
+    @pl.when(core[0] != 0)
+    def _():
+        b[:half] = other
+        b[half:] = whole[:half]
 
 
 def shards(tiles, slot, a, b, c, va, vb, vc):
     wide = lax.axis_size("wide")
     narrow = lax.axis_size("narrow")
     chips = narrow // CORES
-    core = lax.axis_index("narrow") % CORES
+    place_in = lax.axis_index("narrow").astype(jnp.int32)
+    core, chip = place_in % CORES, place_in // CORES
     lead = core == 0
     ib, jb, kb = a.shape[0], b.shape[0], c.shape[0]
     rank = a.shape[1]
@@ -256,8 +312,9 @@
     mults = dict(
         mult_b=step_rate / (narrow * ib * kb), mult_c=step_rate / (narrow * ib * jb)
     )
-    far = in_hbm(tiles)
-    core_arg = core.astype(jnp.int32).reshape(1)
+    far, order = in_hbm(tiles), in_hbm(slot)
+    pos = core.reshape(1), chip.reshape(1)
+    assert chips > 1 and half == kb
 
     def permute(x, where):
         route = []
@@ -306,12 +363,6 @@
             sums.append(functools.reduce(jnp.add, terms) if terms else jnp.zeros_like(got[0]))
         return jnp.where(lead, sums[0], sums[1])
 
-    def around(x):
-        return [permute(x, lambda y, u, t=t: (0, y + t, u)) for t in range(1, chips)]
-
-    def ordered(mine, other):
-        return jnp.where(lead, jnp.concatenate([mine, other], axis=0), jnp.concatenate([other, mine], axis=0))
-
     tile_shape = jax.ShapeDtypeStruct((kb, ib, jb), tiles.dtype)
     block_a, block_b, block_c, share = f32(ib, rank), f32(jb, rank), f32(kb, rank), f32(half + kb, rank)
 
@@ -320,52 +371,76 @@
     def scratch(x):
         return pltpu.VMEM(x.shape, x.dtype)
 
+    slots = pltpu.SMEM(slot.shape, slot.dtype)
     args = a, b, c, va, vb, vc
-    tile, a, b, c, va, bc_gram, keep, send = pl.pallas_call(
-        functools.partial(first_kernel, chips=chips, **mults),
-        out_shape=(tile_shape, block_a, block_b, block_c, block_a, grams, share, share),
-        in_specs=[SMEM, SMEM] + [HBM] * 7,
-        out_specs=(VMEM,) * 8,
-        scratch_shapes=[scratch(x) for x in (block_b, block_c, block_b, block_c)]
-        + [pltpu.SemaphoreType.DMA((4,)), pltpu.SemaphoreType.DMA((6,))],
+    tile, a, b, c, va, bc_gram, now, base, keep, send = pl.pallas_call(
+        functools.partial(first_kernel, **mults),
+        out_shape=(tile_shape, block_a, block_b, block_c, block_a, grams, block_c, block_c, share, share),
+        in_specs=[SMEM] * 2 + [HBM] * 8,
+        out_specs=(VMEM,) * 10,
+        scratch_shapes=[scratch(x) for x in (block_b, block_c, block_b, block_c, block_b, f32(2, STEP, jb, rank))]
+        + [slots, pltpu.SemaphoreType.DMA((4,)), pltpu.SemaphoreType.DMA((7,))],
         compiler_params=GRANT,
-    )(core_arg, slot, far, *map(in_hbm, args))
-    now = jnp.where(lead, b, jnp.pad(c, ((0, jb - kb), (0, 0))))
+    )(*pos, order, far, *map(in_hbm, args))
+    none = jnp.zeros((half, rank), jnp.float32)
+
+    def with_base(keep, send, base):
+        for_b, for_c = jnp.where(chip == 0, base, none), jnp.where(chip == 1, base, none)
+        return (
+            keep + jnp.concatenate([for_b, for_c], axis=0),
+            send + jnp.concatenate([none, for_c], axis=0),
+        )
+
+    def forward(x):
+        return permute(x, lambda y, u: ((SECOND_STRIDE, THIRD_STRIDE)[y], y, u) if y < 2 else None)
+
     for s in range(STRATA):
+        keep, send = with_base(keep, send, base)
         received = swap(send)
+        if s == 0:
+            past = forward(now)
         total = keep + received
-        total, now, tile, a, va, b, c, bc_gram = lax.optimization_barrier(
-            (total, now, tile, a, va, b, c, bc_gram)
-        )
+        if s > 0:
+            bc_gram, terms = pl.pallas_call(
+                functools.partial(terms_kernel, **mults),
+                out_shape=(grams, share),
+                in_specs=[VMEM] * 5,
+                out_specs=(VMEM,) * 2,
+                compiler_params=GRANT,
+            )(*ours, mine, b, c)
+            total = total - terms
+        total, tile, a, va, b, c, bc_gram = lax.optimization_barrier((total, tile, a, va, b, c, bc_gram))
         if s + 1 == STRATA:
             break
         got = onward(total)
-        past = permute(now, lambda y, u: ((SECOND_STRIDE, THIRD_STRIDE)[u], y, u))
         tile, a, va, ata, z = pl.pallas_call(
             functools.partial(window_kernel, scale=scale_a, stratum=s + 1),
             out_shape=(tile_shape, block_a, block_a, grams, f32(kb, jb, rank)),
-            in_specs=[SMEM, HBM] + [VMEM] * 6,
+            in_specs=[HBM] * 2 + [VMEM] * 6,
             out_specs=(VMEM,) * 5,
-            scratch_shapes=[pltpu.SemaphoreType.DMA],
+            scratch_shapes=[slots, pltpu.SemaphoreType.DMA, pltpu.SemaphoreType.DMA],
             compiler_params=GRANT,
-        )(slot, far, tile, a, va, b, c, bc_gram)
-        got, a, va, ata, z = lax.optimization_barrier((got, a, va, ata, z))
+        )(order, far, tile, a, va, b, c, bc_gram)
+        ata_other = swap(ata)
+        got, a, va, z = lax.optimization_barrier((got, a, va, z))
+        ours = ata, ata_other
         mine = jnp.concatenate([collect(got, "b"), collect(got, "c")], axis=0)
         other = swap(mine)
-        b, c, now, bc_gram, keep, send = pl.pallas_call(
+        before = past
+        if s + 2 < STRATA:
+            past = forward(jnp.where(chip == 0, mine[:half], mine[half:]))
+        b, c, keep, send = pl.pallas_call(
             functools.partial(gradient_kernel, **mults),
-            out_shape=(block_b, block_c, block_b, grams, share, share),
-            in_specs=[SMEM] + [VMEM] * 6,
-            out_specs=(VMEM,) * 6,
-            scratch_shapes=[scratch(block_b), scratch(block_c)],
+            out_shape=(block_b, block_c, share, share),
+            in_specs=[SMEM] + [VMEM] * 5,
+            out_specs=(VMEM,) * 4,
+            scratch_shapes=[scratch(x) for x in (block_b, block_c) + (f32(STEP, ib, rank),) * 2],
             compiler_params=GRANT,
-        )(core_arg, tile, z, a, ata, mine, other)
-        base = ((1.0 + momentum) * now - momentum * past) * (1.0 / chips)
-        none = jnp.zeros((half, rank), jnp.float32)
-        for_c = jnp.where(lead, 0.0, base[:kb])
-        keep = keep + jnp.concatenate([jnp.where(lead, base[:half], none), for_c], axis=0)
-        send = send + jnp.concatenate([jnp.where(lead, base[half:], none), for_c], axis=0)
-    others = around(total)
+        )(pos[0], tile, z, a, mine, other)
+        base = (1.0 + momentum) * jnp.where(chip == 0, mine[:half], (1.0 / CORES) * c) - momentum * before
+    beside = swap(total[:half])
+    same = [permute(total, lambda y, u, t=t: (0, y + t, u)) for t in range(1, chips)]
+    cross = [permute(total[:half], lambda y, u, t=t: (0, y + t, u + 1)) for t in range(1, chips)]
     a = pl.pallas_call(
         functools.partial(last_kernel, scale=scale_a),
         out_shape=f32(ib, rank),
@@ -373,9 +448,15 @@
         out_specs=VMEM,
         compiler_params=GRANT,
     )(tile, a, va, b, c, bc_gram)
-    others, a = lax.optimization_barrier((others, a))
-    total = functools.reduce(jnp.add, others, total)
-    return a, ordered(total[:half], swap(total[:half])), total[half:]
+    beside, same, cross, a = lax.optimization_barrier((beside, same, cross, a))
+    b, c = pl.pallas_call(
+        final_kernel,
+        out_shape=(block_b, block_c),
+        in_specs=[SMEM] + [VMEM] * 4,
+        out_specs=(VMEM,) * 2,
+        compiler_params=GRANT,
+    )(pos[0], total, beside, jnp.stack(same), jnp.stack(cross))
+    return a, b, c
 
 
 def solution(mesh):

time: 80.8 us -> 73.4 us (0.908)
  starting transfers between devices: 21.7 us -> 17.2 us
  local copies, waits for them, and re-layouts: 1.94 us -> 0.01 us
    ppermute x21 -> x25, starting transfers between devices: 21.7 us -> 17.2 us  [permute(): return lax.ppermute(x, BOTH, route)]
    unnamed x4 -> x0, local copies, waits for them, and re-layouts: 1.31 us -> none
    pallas_call x3, Pallas kernels: 7 us -> 5.92 us  [shards(): pl.pallas_call(functools.partial(gradient_kernel, **mults), out_shape=(bl...]
    pallas_call x1 -> x5, Pallas kernels: 5.42 us -> 6.06 us  [the longest x1 3.75 us: shards(): pl.pallas_call(functools.partial(first_kernel, **mults), out_shape=(tile_...]
    ppermute x21 -> x25, waiting for transfers between devices: 27.8 us -> 27.7 us  [permute(): return lax.ppermute(x, BOTH, route)]
  transfers between devices with their start and end apart: 21 -> 25, of which waited for: 17 -> 17; matrix products, arithmetic and copies ran while one was open for 0% -> 0% of each run, Pallas kernels for 27% -> 31%
where the time goes in v1:
time: 73.4 us; the launch traced here: 73.2 us
  waiting for transfers between devices  27.7 us (38%)
  Pallas kernels  27 us (37%)
  starting transfers between devices  17.2 us (23%)
  between operations  0.96 us (1%)
    ppermute x25, waiting for transfers between devices, permute(): return lax.ppermute(x, BOTH, route)  27.7 us
    ppermute x25, starting transfers between devices, permute(): return lax.ppermute(x, BOTH, route)  17.2 us
    pallas_call x3, Pallas kernels, shards(): pl.pallas_call(functools.partial(window_kernel, scale=scale_a, stratum=s...  12.9 us
    pallas_call x3, Pallas kernels, shards(): pl.pallas_call(functools.partial(gradient_kernel, **mults), out_shape=(bl...  5.92 us
    pallas_call x1, Pallas kernels, shards(): pl.pallas_call(functools.partial(first_kernel, **mults), out_shape=(tile_...  3.75 us
    pallas_call x1, Pallas kernels, shards(): pl.pallas_call(functools.partial(last_kernel, scale=scale_a), out_shape=f...  2.15 us
    pallas_call x3, Pallas kernels, shards(): pl.pallas_call(functools.partial(terms_kernel, **mults), out_shape=(grams...  1.61 us
  transfers between devices with their start and end apart: 25, of which 17 were waited for; matrix products, arithmetic and copies ran while one was open for 0% of the time, Pallas kernels for 31%

profile of v1, /device:TPU:0, one launch (start us, length us, event | category | flops | bytes accessed | tf_op | source)
XLA Modules:
  0.0 73.2 jit_solution(10596001025362795389)
XLA Ops:
  0.7 3.7 %shard_map.103 = (bf16[64,64,128]{2,1,0:T(8,128)(2,1)S(1)}, f32[64,256]{1,0:T(8,128)S(1)}, f32[128,256]{1,0:T(8,128)S(1)}, f32[64,256]{1,0:T(8,128)S(1)}, f32[64...) custom-call(s32[1]{0:T(128)} %bitcast.core, ...), custom_call_target="tpu_custom_call" | custom-call | tf_op jit(solution)/shard_map/pallas_call | solution.py:376
  4.5 0.6 collective-permute-start
  5.0 1.0 %collective-permute-done = f32[128,256]{1,0:T(8,128)S(1)} collective-permute-done((f32[128,256]{1,0:T(8,128)S(1)}, f32[128,256]{1,0:T(8,128)S(1)}, u32[]{:S(2)}, u32[]{:S(2)}) %collective-permute-start) | collective-permute-done | bytes 131104 | tf_op jit(solution)/shard_map/ppermute | solution.py:328
  6.1 2.9 %collective-permute-start.1 = (f32[64,256]{1,0:T(8,128)S(1)}, f32[64,256]{1,0:T(8,128)S(1)}, u32[]{:S(2)}, u32[]{:S(2)}) collective-permute-start(f32[64,256]{1,0:T(8,128)S(1)} %get-tuple-element.214), channel_id=1, source_target_pairs={{0,4},{1,15},{2,6},{3,13},{4,8},{5,19},{6,10},{7,17},{8,12},{9,23}... | collective-permute-start | bytes 196616 | tf_op jit(solution)/shard_map/ppermute | solution.py:328
  8.9 2.5 %collective-permute-start.2 = (f32[64,256]{1,0:T(8,128)S(1)}, f32[64,256]{1,0:T(8,128)S(1)}, u32[]{:S(2)}, u32[]{:S(2)}) collective-permute-start(f32[64,256]{1,0:T(8,128)S(1)} %get-tuple-element.215), channel_id=1, source_target_pairs={{0,6},{1,5},{2,4},{3,7},{4,10},{5,9},{6,8},{7,11},{8,14},{9,13},{1... | collective-permute-start | bytes 196616 | tf_op jit(solution)/shard_map/ppermute | solution.py:328
  11.4 2.5 %collective-permute-start.3 = (f32[64,256]{1,0:T(8,128)S(1)}, f32[64,256]{1,0:T(8,128)S(1)}, u32[]{:S(2)}, u32[]{:S(2)}) collective-permute-start(f32[64,256]{1,0:T(8,128)S(1)} %get-tuple-element.213), channel_id=1, source_target_pairs={{0,12},{1,7},{2,14},{3,5},{4,16},{5,11},{6,18},{7,9},{8,20},{9,15}... | collective-permute-start | bytes 196616 | tf_op jit(solution)/shard_map/ppermute | solution.py:328
  14.0 4.3 %shard_map.104 = (bf16[64,64,128]{2,1,0:T(8,128)(2,1)S(1)}, f32[64,256]{1,0:T(8,128)S(1)}, f32[64,256]{1,0:T(8,128)S(1)}, f32[256,256]{1,0:T(8,128)S(1)}, f32[64,128,256]{2,1,0:T(8,128)S(1)}) custom-call(s32[1,4]{1,0:T(1,128)} %slot_in.7, bf16[4,64,64,128]{3,2,1,0:T(8,128)(2,1)} %tiles.7, bf16[64,64,128]{2,1,0:T(8,128)(2,1)S(1)} %get-tuple-element.107.old, ...), custom_call_target="tpu_custom_call" | custom-call | tf_op jit(solution)/shard_map/pallas_call | solution.py:416
  18.3 0.0 collective-permute-done.1
  18.3 0.0 collective-permute-done.2
  18.3 1.3 %collective-permute-done.3 = f32[64,256]{1,0:T(8,128)S(1)} collective-permute-done((f32[64,256]{1,0:T(8,128)S(1)}, f32[64,256]{1,0:T(8,128)S(1)}, u32[]{:S(2)}, u32[]{:S(2)}) %collective-permute-start.3) | collective-permute-done | bytes 65568 | tf_op jit(solution)/shard_map/ppermute | solution.py:328
  19.6 0.1 collective-permute-start.4
  19.7 0.4 collective-permute-start.5
  20.1 0.2 collective-permute-start.7
  20.2 0.8 %collective-permute-done.4.other = f32[128,256]{1,0:T(8,128)S(1)} collective-permute-done((f32[128,256]{1,0:T(8,128)S(1)}, f32[128,256]{1,0:T(8,128)S(1)}, u32[]{:S(2)}, u32[]{:S(2)}) %collective-permute-start.4) | collective-permute-done | bytes 131104 | tf_op jit(solution)/shard_map/ppermute | solution.py:328
  21.0 2.0 %shard_map.105 = (f32[128,256]{1,0:T(8,128)S(1)}, f32[64,256]{1,0:T(8,128)S(1)}, f32[128,256]{1,0:T(8,128)S(1)}, f32[128,256]{1,0:T(8,128)S(1)}) custom-call(s32[1]{0:T(128)} %bitcast.core, bf16[64,64,128]{2,1,0:T(8,128)(2,1)S(1)} %get-tuple-element.132.tile.old, f32[64,128,256]{2,1,0:T(8,128)S(1)} %get-tuple-element.118.z, ...), custom_call_target="tpu_custom_call" | custom-call | tf_op jit(solution)/shard_map/pallas_call | solution.py:432
  23.0 3.9 %collective-permute-done.5 = f32[64,256]{1,0:T(8,128)S(1)} collective-permute-done((f32[64,256]{1,0:T(8,128)S(1)}, f32[64,256]{1,0:T(8,128)S(1)}, u32[]{:S(2)}, u32[]{:S(2)}) %collective-permute-start.5) | collective-permute-done | bytes 65568 | tf_op jit(solution)/shard_map/ppermute | solution.py:328
  26.9 0.1 collective-permute-start.6
  27.0 0.0 collective-permute-done.7.ata_other
  27.0 0.5 shard_map.106
  27.6 0.8 %collective-permute-done.6 = f32[128,256]{1,0:T(8,128)S(1)} collective-permute-done((f32[128,256]{1,0:T(8,128)S(1)}, f32[128,256]{1,0:T(8,128)S(1)}, u32[]{:S(2)}, u32[]{:S(2)}) %collective-permute-start.6) | collective-permute-done | bytes 131104 | tf_op jit(solution)/shard_map/ppermute | solution.py:328
  28.4 0.1 collective-permute-start.10
  28.5 0.7 collective-permute-start.8
  29.2 1.2 %collective-permute-start.9 = (f32[64,256]{1,0:T(8,128)S(1)}, f32[64,256]{1,0:T(8,128)S(1)}, u32[]{:S(2)}, u32[]{:S(2)}) collective-permute-start(f32[64,256]{1,0:T(8,128)S(1)} %get-tuple-element.212), channel_id=1, source_target_pairs={{0,6},{1,5},{2,4},{3,7},{4,10},{5,9},{6,8},{7,11},{8,14},{9,13},{1... | collective-permute-start | bytes 196616 | tf_op jit(solution)/shard_map/ppermute | solution.py:328
  30.4 4.3 %shard_map.107 = (bf16[64,64,128]{2,1,0:T(8,128)(2,1)S(1)}, f32[64,256]{1,0:T(8,128)S(1)}, f32[64,256]{1,0:T(8,128)S(1)}, f32[256,256]{1,0:T(8,128)S(1)}, f32[64,128,256]{2,1,0:T(8,128)S(1)}) custom-call(s32[1,4]{1,0:T(1,128)} %slot_in.7, bf16[4,64,64,128]{3,2,1,0:T(8,128)(2,1)} %tiles.7, bf16[64,64,128]{2,1,0:T(8,128)(2,1)S(1)} %get-tuple-element.132.tile.old, ...), custom_call_target="tpu_custom_call" | custom-call | tf_op jit(solution)/shard_map/pallas_call | solution.py:416
  34.7 3.5 %collective-permute-done.10 = f32[64,256]{1,0:T(8,128)S(1)} collective-permute-done((f32[64,256]{1,0:T(8,128)S(1)}, f32[64,256]{1,0:T(8,128)S(1)}, u32[]{:S(2)}, u32[]{:S(2)}) %collective-permute-start.10) | collective-permute-done | bytes 65568 | tf_op jit(solution)/shard_map/ppermute | solution.py:328
  38.2 0.0 collective-permute-done.8
  38.2 0.0 collective-permute-done.9
  38.2 0.6 collective-permute-start.11
  38.8 0.2 collective-permute-start.12
  39.0 0.2 collective-permute-start.14
  39.2 0.6 collective-permute-done.11.other
  39.8 2.0 %shard_map.108 = (f32[128,256]{1,0:T(8,128)S(1)}, f32[64,256]{1,0:T(8,128)S(1)}, f32[128,256]{1,0:T(8,128)S(1)}, f32[128,256]{1,0:T(8,128)S(1)}) custom-call(s32[1]{0:T(128)} %bitcast.core, bf16[64,64,128]{2,1,0:T(8,128)(2,1)S(1)} %get-tuple-element.156.tile.old, f32[64,128,256]{2,1,0:T(8,128)S(1)} %get-tuple-element.143.z, ...), custom_call_target="tpu_custom_call" | custom-call | tf_op jit(solution)/shard_map/pallas_call | solution.py:432
  41.8 4.0 %collective-permute-done.12 = f32[64,256]{1,0:T(8,128)S(1)} collective-permute-done((f32[64,256]{1,0:T(8,128)S(1)}, f32[64,256]{1,0:T(8,128)S(1)}, u32[]{:S(2)}, u32[]{:S(2)}) %collective-permute-start.12) | collective-permute-done | bytes 65568 | tf_op jit(solution)/shard_map/ppermute | solution.py:328
  45.8 0.1 collective-permute-start.13
  45.9 0.0 collective-permute-done.14.ata_other
  45.9 0.5 shard_map.109
  46.4 0.8 %collective-permute-done.13 = f32[128,256]{1,0:T(8,128)S(1)} collective-permute-done((f32[128,256]{1,0:T(8,128)S(1)}, f32[128,256]{1,0:T(8,128)S(1)}, u32[]{:S(2)}, u32[]{:S(2)}) %collective-permute-start.13) | collective-permute-done | bytes 131104 | tf_op jit(solution)/shard_map/ppermute | solution.py:328
  47.3 0.1 collective-permute-start.15
  47.4 1.3 %collective-permute-start.16 = (f32[64,256]{1,0:T(8,128)S(1)}, f32[64,256]{1,0:T(8,128)S(1)}, u32[]{:S(2)}, u32[]{:S(2)}) collective-permute-start(f32[64,256]{1,0:T(8,128)S(1)} %get-tuple-element.209), channel_id=1, source_target_pairs={{0,6},{1,5},{2,4},{3,7},{4,10},{5,9},{6,8},{7,11},{8,14},{9,13},{1... | collective-permute-start | bytes 196616 | tf_op jit(solution)/shard_map/ppermute | solution.py:328
  48.7 0.9 %collective-permute-start.17 = (f32[64,256]{1,0:T(8,128)S(1)}, f32[64,256]{1,0:T(8,128)S(1)}, u32[]{:S(2)}, u32[]{:S(2)}) collective-permute-start(f32[64,256]{1,0:T(8,128)S(1)} %get-tuple-element.207), channel_id=1, source_target_pairs={{0,12},{1,7},{2,14},{3,5},{4,16},{5,11},{6,18},{7,9},{8,20},{9,15}... | collective-permute-start | bytes 196616 | tf_op jit(solution)/shard_map/ppermute | solution.py:328
  49.5 4.3 %shard_map.110 = (bf16[64,64,128]{2,1,0:T(8,128)(2,1)S(1)}, f32[64,256]{1,0:T(8,128)S(1)}, f32[64,256]{1,0:T(8,128)S(1)}, f32[256,256]{1,0:T(8,128)S(1)}, f32[64,128,256]{2,1,0:T(8,128)S(1)}) custom-call(s32[1,4]{1,0:T(1,128)} %slot_in.7, bf16[4,64,64,128]{3,2,1,0:T(8,128)(2,1)} %tiles.7, bf16[64,64,128]{2,1,0:T(8,128)(2,1)S(1)} %get-tuple-element.156.tile.old, ...), custom_call_target="tpu_custom_call" | custom-call | tf_op jit(solution)/shard_map/pallas_call | solution.py:416
  53.8 1.2 %collective-permute-done.15 = f32[64,256]{1,0:T(8,128)S(1)} collective-permute-done((f32[64,256]{1,0:T(8,128)S(1)}, f32[64,256]{1,0:T(8,128)S(1)}, u32[]{:S(2)}, u32[]{:S(2)}) %collective-permute-start.15) | collective-permute-done | bytes 65568 | tf_op jit(solution)/shard_map/ppermute | solution.py:328
  55.0 1.3 %collective-permute-done.16 = f32[64,256]{1,0:T(8,128)S(1)} collective-permute-done((f32[64,256]{1,0:T(8,128)S(1)}, f32[64,256]{1,0:T(8,128)S(1)}, u32[]{:S(2)}, u32[]{:S(2)}) %collective-permute-start.16) | collective-permute-done | bytes 65568 | tf_op jit(solution)/shard_map/ppermute | solution.py:328
  56.3 1.0 %collective-permute-done.17 = f32[64,256]{1,0:T(8,128)S(1)} collective-permute-done((f32[64,256]{1,0:T(8,128)S(1)}, f32[64,256]{1,0:T(8,128)S(1)}, u32[]{:S(2)}, u32[]{:S(2)}) %collective-permute-start.17) | collective-permute-done | bytes 65568 | tf_op jit(solution)/shard_map/ppermute | solution.py:328
  57.4 0.1 collective-permute-start.18
  57.5 0.1 collective-permute-start.19
  57.6 0.4 collective-permute-start.21
  58.0 0.8 %collective-permute-done.18.other = f32[128,256]{1,0:T(8,128)S(1)} collective-permute-done((f32[128,256]{1,0:T(8,128)S(1)}, f32[128,256]{1,0:T(8,128)S(1)}, u32[]{:S(2)}, u32[]{:S(2)}) %collective-permute-start.18) | collective-permute-done | bytes 131104 | tf_op jit(solution)/shard_map/ppermute | solution.py:328
  58.8 2.0 %shard_map.111 = (f32[128,256]{1,0:T(8,128)S(1)}, f32[64,256]{1,0:T(8,128)S(1)}, f32[128,256]{1,0:T(8,128)S(1)}, f32[128,256]{1,0:T(8,128)S(1)}) custom-call(s32[1]{0:T(128)} %bitcast.core, bf16[64,64,128]{2,1,0:T(8,128)(2,1)S(1)} %get-tuple-element.181.tile.old, f32[64,128,256]{2,1,0:T(8,128)S(1)} %get-tuple-element.167.z, ...), custom_call_target="tpu_custom_call" | custom-call | tf_op jit(solution)/shard_map/pallas_call | solution.py:432
  60.8 3.9 %collective-permute-done.19 = f32[64,256]{1,0:T(8,128)S(1)} collective-permute-done((f32[64,256]{1,0:T(8,128)S(1)}, f32[64,256]{1,0:T(8,128)S(1)}, u32[]{:S(2)}, u32[]{:S(2)}) %collective-permute-start.19) | collective-permute-done | bytes 65568 | tf_op jit(solution)/shard_map/ppermute | solution.py:328
  64.7 0.1 collective-permute-start.20
  64.8 0.0 collective-permute-done.21.ata_other
  64.8 0.5 shard_map.112
  65.4 0.8 %collective-permute-done.20 = f32[128,256]{1,0:T(8,128)S(1)} collective-permute-done((f32[128,256]{1,0:T(8,128)S(1)}, f32[128,256]{1,0:T(8,128)S(1)}, u32[]{:S(2)}, u32[]{:S(2)}) %collective-permute-start.20) | collective-permute-done | bytes 131104 | tf_op jit(solution)/shard_map/ppermute | solution.py:328
  66.2 0.8 %collective-permute-start.23 = (f32[128,256]{1,0:T(8,128)S(1)}, f32[128,256]{1,0:T(8,128)S(1)}, u32[]{:S(2)}, u32[]{:S(2)}) collective-permute-start(f32[128,256]{1,0:T(8,128)S(1)} %fusion.6.total), channel_id=1, source_target_pairs={{0,2},{1,3},{2,0},{3,1},{4,6},{5,7},{6,4},{7,5},{8,10},{9,11},{10,... | collective-permute-start | bytes 393224 | tf_op jit(solution)/shard_map/ppermute | solution.py:328
  67.0 0.0 collective-permute-start.22
  67.0 1.4 %collective-permute-start.24 = (f32[64,256]{1,0:T(8,128)S(1)}, f32[64,256]{1,0:T(8,128)S(1)}, u32[]{:S(2)}, u32[]{:S(2)}) collective-permute-start(f32[64,256]{1,0:T(8,128)S(1)} %slice.28), channel_id=1, source_target_pairs={{0,3},{1,2},{2,1},{3,0},{4,7},{5,6},{6,5},{7,4},{8,11},{9,10},{10,... | collective-permute-start | bytes 196616 | tf_op jit(solution)/shard_map/ppermute | solution.py:328
  68.4 2.1 %shard_map.113 = f32[64,256]{1,0:T(8,128)} custom-call(bf16[64,64,128]{2,1,0:T(8,128)(2,1)S(1)} %get-tuple-element.181.tile.old, f32[64,256]{1,0:T(8,128)S(1)} %get-tuple-element.182.a, f32[64,256]{1,0:T(8,128)S(1)} %get-tuple-element.183.va, f32[128,256]{1,0:T(8,128)S(1)} %get-tuple-element.184.b, f32[64,256]{1,0:T(8,128)S(1)} %get-tuple-element.185.c, ...), custom_call_target="tpu_custom_call" | custom-call | tf_op jit(solution)/shard_map/pallas_call | solution.py:444
  70.6 0.0 collective-permute-done.22.beside
  70.6 1.8 %collective-permute-done.24 = f32[64,256]{1,0:T(8,128)S(1)} collective-permute-done((f32[64,256]{1,0:T(8,128)S(1)}, f32[64,256]{1,0:T(8,128)S(1)}, u32[]{:S(2)}, u32[]{:S(2)}) %collective-permute-start.24) | collective-permute-done | bytes 65568 | tf_op jit(solution)/shard_map/ppermute | solution.py:328
  72.4 0.1 collective-permute-done.23
  72.5 0.7 shard_map.114
  (22 shorter events, 0.4 us)
Async XLA Ops:
  4.5 1.5 %collective-permute-start = (f32[128,256]{1,0:T(8,128)S(1)}, f32[128,256]{1,0:T(8,128)S(1)}, u32[]{:S(2)}, u32[]{:S(2)}) collective-permute-start(f32[128,256]{1,0:T(8,128)S(1)} %pad_add_fusion.3), channel_id=1, source_target_pairs={{0,1},{1,0},{2,3},{3,2},{4,5},{5,4},{6,7},{7,6},{8,9},{9,8},{10,11... | collective-permute-start | bytes 393224 | tf_op jit(solution)/shard_map/ppermute | solution.py:328
  6.1 12.2 %collective-permute-start.1 = (f32[64,256]{1,0:T(8,128)S(1)}, f32[64,256]{1,0:T(8,128)S(1)}, u32[]{:S(2)}, u32[]{:S(2)}) collective-permute-start(f32[64,256]{1,0:T(8,128)S(1)} %get-tuple-element.214), channel_id=1, source_target_pairs={{0,4},{1,15},{2,6},{3,13},{4,8},{5,19},{6,10},{7,17},{8,12},{9,23}... | collective-permute-start | bytes 196616 | tf_op jit(solution)/shard_map/ppermute | solution.py:328
  8.9 9.3 %collective-permute-start.2 = (f32[64,256]{1,0:T(8,128)S(1)}, f32[64,256]{1,0:T(8,128)S(1)}, u32[]{:S(2)}, u32[]{:S(2)}) collective-permute-start(f32[64,256]{1,0:T(8,128)S(1)} %get-tuple-element.215), channel_id=1, source_target_pairs={{0,6},{1,5},{2,4},{3,7},{4,10},{5,9},{6,8},{7,11},{8,14},{9,13},{1... | collective-permute-start | bytes 196616 | tf_op jit(solution)/shard_map/ppermute | solution.py:328
  11.4 8.1 %collective-permute-start.3 = (f32[64,256]{1,0:T(8,128)S(1)}, f32[64,256]{1,0:T(8,128)S(1)}, u32[]{:S(2)}, u32[]{:S(2)}) collective-permute-start(f32[64,256]{1,0:T(8,128)S(1)} %get-tuple-element.213), channel_id=1, source_target_pairs={{0,12},{1,7},{2,14},{3,5},{4,16},{5,11},{6,18},{7,9},{8,20},{9,15}... | collective-permute-start | bytes 196616 | tf_op jit(solution)/shard_map/ppermute | solution.py:328
  19.6 1.4 %collective-permute-start.4 = (f32[128,256]{1,0:T(8,128)S(1)}, f32[128,256]{1,0:T(8,128)S(1)}, u32[]{:S(2)}, u32[]{:S(2)}) collective-permute-start(f32[128,256]{1,0:T(8,128)S(1)} %pad_maximum_fusion.mine), channel_id=1, source_target_pairs={{0,1},{1,0},{2,3},{3,2},{4,5},{5,4},{6,7},{7,6},{8,9},{9,8},{10,11... | collective-permute-start | bytes 393224 | tf_op jit(solution)/shard_map/ppermute | solution.py:328
  19.7 7.2 %collective-permute-start.5 = (f32[64,256]{1,0:T(8,128)S(1)}, f32[64,256]{1,0:T(8,128)S(1)}, u32[]{:S(2)}, u32[]{:S(2)}) collective-permute-start(f32[64,256]{1,0:T(8,128)S(1)} %get-tuple-element.125), channel_id=1, source_target_pairs={{0,4},{1,5},{2,14},{3,15},{4,8},{5,9},{6,18},{7,19},{8,12},{9,13},... | collective-permute-start | bytes 196616 | tf_op jit(solution)/shard_map/ppermute | solution.py:328
  20.1 6.9 %collective-permute-start.7 = (f32[256,256]{1,0:T(8,128)S(1)}, f32[256,256]{1,0:T(8,128)S(1)}, u32[]{:S(2)}, u32[]{:S(2)}) collective-permute-start(f32[256,256]{1,0:T(8,128)S(1)} %get-tuple-element.127.ata), channel_id=1, source_target_pairs={{0,1},{1,0},{2,3},{3,2},{4,5},{5,4},{6,7},{7,6},{8,9},{9,8},{10,11... | collective-permute-start | bytes 786440 | tf_op jit(solution)/shard_map/ppermute | solution.py:328
  26.9 1.4 %collective-permute-start.6 = (f32[128,256]{1,0:T(8,128)S(1)}, f32[128,256]{1,0:T(8,128)S(1)}, u32[]{:S(2)}, u32[]{:S(2)}) collective-permute-start(f32[128,256]{1,0:T(8,128)S(1)} %pad_add_fusion.2), channel_id=1, source_target_pairs={{0,1},{1,0},{2,3},{3,2},{4,5},{5,4},{6,7},{7,6},{8,9},{9,8},{10,11... | collective-permute-start | bytes 393224 | tf_op jit(solution)/shard_map/ppermute | solution.py:328
  28.4 9.7 %collective-permute-start.10 = (f32[64,256]{1,0:T(8,128)S(1)}, f32[64,256]{1,0:T(8,128)S(1)}, u32[]{:S(2)}, u32[]{:S(2)}) collective-permute-start(f32[64,256]{1,0:T(8,128)S(1)} %get-tuple-element.210), channel_id=1, source_target_pairs={{0,12},{1,7},{2,14},{3,5},{4,16},{5,11},{6,18},{7,9},{8,20},{9,15}... | collective-permute-start | bytes 196616 | tf_op jit(solution)/shard_map/ppermute | solution.py:328
  28.5 9.7 %collective-permute-start.8 = (f32[64,256]{1,0:T(8,128)S(1)}, f32[64,256]{1,0:T(8,128)S(1)}, u32[]{:S(2)}, u32[]{:S(2)}) collective-permute-start(f32[64,256]{1,0:T(8,128)S(1)} %get-tuple-element.211), channel_id=1, source_target_pairs={{0,4},{1,15},{2,6},{3,13},{4,8},{5,19},{6,10},{7,17},{8,12},{9,23}... | collective-permute-start | bytes 196616 | tf_op jit(solution)/shard_map/ppermute | solution.py:328
  29.2 9.0 %collective-permute-start.9 = (f32[64,256]{1,0:T(8,128)S(1)}, f32[64,256]{1,0:T(8,128)S(1)}, u32[]{:S(2)}, u32[]{:S(2)}) collective-permute-start(f32[64,256]{1,0:T(8,128)S(1)} %get-tuple-element.212), channel_id=1, source_target_pairs={{0,6},{1,5},{2,4},{3,7},{4,10},{5,9},{6,8},{7,11},{8,14},{9,13},{1... | collective-permute-start | bytes 196616 | tf_op jit(solution)/shard_map/ppermute | solution.py:328
  38.2 1.6 %collective-permute-start.11 = (f32[128,256]{1,0:T(8,128)S(1)}, f32[128,256]{1,0:T(8,128)S(1)}, u32[]{:S(2)}, u32[]{:S(2)}) collective-permute-start(f32[128,256]{1,0:T(8,128)S(1)} %pad_maximum_fusion.1.mine), channel_id=1, source_target_pairs={{0,1},{1,0},{2,3},{3,2},{4,5},{5,4},{6,7},{7,6},{8,9},{9,8},{10,11... | collective-permute-start | bytes 393224 | tf_op jit(solution)/shard_map/ppermute | solution.py:328
  38.8 7.0 %collective-permute-start.12 = (f32[64,256]{1,0:T(8,128)S(1)}, f32[64,256]{1,0:T(8,128)S(1)}, u32[]{:S(2)}, u32[]{:S(2)}) collective-permute-start(f32[64,256]{1,0:T(8,128)S(1)} %get-tuple-element.196), channel_id=1, source_target_pairs={{0,4},{1,5},{2,14},{3,15},{4,8},{5,9},{6,18},{7,19},{8,12},{9,13},... | collective-permute-start | bytes 196616 | tf_op jit(solution)/shard_map/ppermute | solution.py:328
  39.0 6.9 %collective-permute-start.14 = (f32[256,256]{1,0:T(8,128)S(1)}, f32[256,256]{1,0:T(8,128)S(1)}, u32[]{:S(2)}, u32[]{:S(2)}) collective-permute-start(f32[256,256]{1,0:T(8,128)S(1)} %get-tuple-element.151.ata), channel_id=1, source_target_pairs={{0,1},{1,0},{2,3},{3,2},{4,5},{5,4},{6,7},{7,6},{8,9},{9,8},{10,11... | collective-permute-start | bytes 786440 | tf_op jit(solution)/shard_map/ppermute | solution.py:328
  45.8 1.4 %collective-permute-start.13 = (f32[128,256]{1,0:T(8,128)S(1)}, f32[128,256]{1,0:T(8,128)S(1)}, u32[]{:S(2)}, u32[]{:S(2)}) collective-permute-start(f32[128,256]{1,0:T(8,128)S(1)} %pad_add_fusion.1), channel_id=1, source_target_pairs={{0,1},{1,0},{2,3},{3,2},{4,5},{5,4},{6,7},{7,6},{8,9},{9,8},{10,11... | collective-permute-start | bytes 393224 | tf_op jit(solution)/shard_map/ppermute | solution.py:328
  47.3 7.7 %collective-permute-start.15 = (f32[64,256]{1,0:T(8,128)S(1)}, f32[64,256]{1,0:T(8,128)S(1)}, u32[]{:S(2)}, u32[]{:S(2)}) collective-permute-start(f32[64,256]{1,0:T(8,128)S(1)} %get-tuple-element.208), channel_id=1, source_target_pairs={{0,4},{1,15},{2,6},{3,13},{4,8},{5,19},{6,10},{7,17},{8,12},{9,23}... | collective-permute-start | bytes 196616 | tf_op jit(solution)/shard_map/ppermute | solution.py:328
  47.4 9.0 %collective-permute-start.16 = (f32[64,256]{1,0:T(8,128)S(1)}, f32[64,256]{1,0:T(8,128)S(1)}, u32[]{:S(2)}, u32[]{:S(2)}) collective-permute-start(f32[64,256]{1,0:T(8,128)S(1)} %get-tuple-element.209), channel_id=1, source_target_pairs={{0,6},{1,5},{2,4},{3,7},{4,10},{5,9},{6,8},{7,11},{8,14},{9,13},{1... | collective-permute-start | bytes 196616 | tf_op jit(solution)/shard_map/ppermute | solution.py:328
  48.7 8.7 %collective-permute-start.17 = (f32[64,256]{1,0:T(8,128)S(1)}, f32[64,256]{1,0:T(8,128)S(1)}, u32[]{:S(2)}, u32[]{:S(2)}) collective-permute-start(f32[64,256]{1,0:T(8,128)S(1)} %get-tuple-element.207), channel_id=1, source_target_pairs={{0,12},{1,7},{2,14},{3,5},{4,16},{5,11},{6,18},{7,9},{8,20},{9,15}... | collective-permute-start | bytes 196616 | tf_op jit(solution)/shard_map/ppermute | solution.py:328
  57.4 1.4 %collective-permute-start.18 = (f32[128,256]{1,0:T(8,128)S(1)}, f32[128,256]{1,0:T(8,128)S(1)}, u32[]{:S(2)}, u32[]{:S(2)}) collective-permute-start(f32[128,256]{1,0:T(8,128)S(1)} %pad_maximum_fusion.2.mine), channel_id=1, source_target_pairs={{0,1},{1,0},{2,3},{3,2},{4,5},{5,4},{6,7},{7,6},{8,9},{9,8},{10,11... | collective-permute-start | bytes 393224 | tf_op jit(solution)/shard_map/ppermute | solution.py:328
  57.5 7.2 %collective-permute-start.19 = (f32[64,256]{1,0:T(8,128)S(1)}, f32[64,256]{1,0:T(8,128)S(1)}, u32[]{:S(2)}, u32[]{:S(2)}) collective-permute-start(f32[64,256]{1,0:T(8,128)S(1)} %get-tuple-element.193), channel_id=1, source_target_pairs={{0,4},{1,5},{2,14},{3,15},{4,8},{5,9},{6,18},{7,19},{8,12},{9,13},... | collective-permute-start | bytes 196616 | tf_op jit(solution)/shard_map/ppermute | solution.py:328
  57.6 7.3 %collective-permute-start.21 = (f32[256,256]{1,0:T(8,128)S(1)}, f32[256,256]{1,0:T(8,128)S(1)}, u32[]{:S(2)}, u32[]{:S(2)}) collective-permute-start(f32[256,256]{1,0:T(8,128)S(1)} %get-tuple-element.175.ata), channel_id=1, source_target_pairs={{0,1},{1,0},{2,3},{3,2},{4,5},{5,4},{6,7},{7,6},{8,9},{9,8},{10,11... | collective-permute-start | bytes 786440 | tf_op jit(solution)/shard_map/ppermute | solution.py:328
  64.7 1.4 %collective-permute-start.20 = (f32[128,256]{1,0:T(8,128)S(1)}, f32[128,256]{1,0:T(8,128)S(1)}, u32[]{:S(2)}, u32[]{:S(2)}) collective-permute-start(f32[128,256]{1,0:T(8,128)S(1)} %pad_add_fusion), channel_id=1, source_target_pairs={{0,1},{1,0},{2,3},{3,2},{4,5},{5,4},{6,7},{7,6},{8,9},{9,8},{10,11... | collective-permute-start | bytes 393224 | tf_op jit(solution)/shard_map/ppermute | solution.py:328
  66.2 6.3 %collective-permute-start.23 = (f32[128,256]{1,0:T(8,128)S(1)}, f32[128,256]{1,0:T(8,128)S(1)}, u32[]{:S(2)}, u32[]{:S(2)}) collective-permute-start(f32[128,256]{1,0:T(8,128)S(1)} %fusion.6.total), channel_id=1, source_target_pairs={{0,2},{1,3},{2,0},{3,1},{4,6},{5,7},{6,4},{7,5},{8,10},{9,11},{10,... | collective-permute-start | bytes 393224 | tf_op jit(solution)/shard_map/ppermute | solution.py:328
  67.0 3.6 %collective-permute-start.22 = (f32[64,256]{1,0:T(8,128)S(1)}, f32[64,256]{1,0:T(8,128)S(1)}, u32[]{:S(2)}, u32[]{:S(2)}) collective-permute-start(f32[64,256]{1,0:T(8,128)S(1)} %slice.28), channel_id=1, source_target_pairs={{0,1},{1,0},{2,3},{3,2},{4,5},{5,4},{6,7},{7,6},{8,9},{9,8},{10,11... | collective-permute-start | bytes 196616 | tf_op jit(solution)/shard_map/ppermute | solution.py:328
  67.0 5.4 %collective-permute-start.24 = (f32[64,256]{1,0:T(8,128)S(1)}, f32[64,256]{1,0:T(8,128)S(1)}, u32[]{:S(2)}, u32[]{:S(2)}) collective-permute-start(f32[64,256]{1,0:T(8,128)S(1)} %slice.28), channel_id=1, source_target_pairs={{0,3},{1,2},{2,1},{3,0},{4,7},{5,6},{6,5},{7,4},{8,11},{9,10},{10,... | collective-permute-start | bytes 196616 | tf_op jit(solution)/shard_map/ppermute | solution.py:328

commit v2 on v1

--- a/solution.py
+++ b/solution.py
@@ -85,7 +85,7 @@
     return dot(doubled(x), stacked).reshape(STEP, ib, stacked.shape[1])
 
 
-def advance_a(tile, a, va, b, c, bc_gram, scale):
+def advance_a(tile, a, va, b, c, bc_gram, scale, midway=None):
     kb, ib, _ = tile.shape
     stacked = split_rows(b[...])
 
@@ -97,7 +97,11 @@
             acc = acc + y[m] * cs[m : m + 1]
         return acc
 
-    seen = lax.fori_loop(0, kb // STEP, body, jnp.zeros((ib, a.shape[1]), jnp.float32), unroll=2)
+    early = 2
+    seen = lax.fori_loop(0, early, body, jnp.zeros((ib, a.shape[1]), jnp.float32), unroll=2)
+    if midway is not None:
+        midway()
+    seen = lax.fori_loop(early, kb // STEP, body, seen, unroll=2)
     grad = apply(a[...], bc_gram[...]) - seen
     va_new = momentum * va[...] + grad * scale
     return a[...] - step_rate * va_new, va_new
@@ -108,15 +112,17 @@
 ):
     order = pltpu.make_async_copy(slot_in, slot, slot_sem)
     order.start()
-    order.wait()
-    copy = pltpu.make_async_copy(tiles.at[slot[0, stratum]], new, sem)
-    copy.start()
-    a_new, va_new = advance_a(old, a, va, b, c, bc_gram, scale)
+
+    def fetch():
+        order.wait()
+        pltpu.make_async_copy(tiles.at[slot[0, stratum]], new, sem).start()
+
+    a_new, va_new = advance_a(old, a, va, b, c, bc_gram, scale, fetch)
     a_out[...] = a_new
     va_out[...] = va_new
     ata[...] = gram(a_new)
     weights = pair_weights(a_new)
-    copy.wait()
+    pltpu.make_async_copy(tiles.at[slot[0, stratum]], new, sem).wait()
 
     def body(n, carry):
         at = pl.multiple_of(n * STEP, STEP)
@@ -124,7 +130,7 @@
             z[at + m] = zk
         return carry
 
-    lax.fori_loop(0, new.shape[0] // STEP, body, 0, unroll=2)
+    lax.fori_loop(0, new.shape[0] // STEP, body, 0, unroll=4)
 
 
 def last_kernel(old, a, va, b, c, bc_gram, a_out, *, scale):
@@ -266,7 +272,7 @@
         return carry
 
     y_even[...] = slices_times_b(tile, 0, stacked)
-    lax.fori_loop(0, steps // 2, body, 0)
+    lax.fori_loop(0, steps // 2, body, 0, unroll=2)
     place(core, mult_b * mb[...], mult_c * mc[...], keep, send)
 
 

time: 73.4 us -> 73.1 us (level)
  waiting for transfers between devices: 27.7 us -> 30.6 us
  Pallas kernels: 27 us -> 24.1 us
    ppermute x25, waiting for transfers between devices: 27.7 us -> 30.6 us  [permute(): return lax.ppermute(x, BOTH, route)]
    pallas_call x3, Pallas kernels: 12.9 us -> 10.8 us  [shards(): pl.pallas_call(functools.partial(window_kernel, scale=scale_a, stratum=s...]
  transfers between devices with their start and end apart: 25 -> 25, of which waited for: 17 -> 17; matrix products, arithmetic and copies ran while one was open for 0% -> 0% of each run, Pallas kernels for 31% -> 27%
where the time goes in v2:
time: 73.1 us; the launch traced here: 72.9 us
  waiting for transfers between devices  30.6 us (42%)
  Pallas kernels  24.1 us (33%)
  starting transfers between devices  16.8 us (23%)
  between operations  0.96 us (1%)
    ppermute x25, waiting for transfers between devices, permute(): return lax.ppermute(x, BOTH, route)  30.6 us
    ppermute x25, starting transfers between devices, permute(): return lax.ppermute(x, BOTH, route)  16.8 us
    pallas_call x3, Pallas kernels, shards(): pl.pallas_call(functools.partial(window_kernel, scale=scale_a, stratum=s...  10.8 us
    pallas_call x3, Pallas kernels, shards(): pl.pallas_call(functools.partial(gradient_kernel, **mults), out_shape=(bl...  5.19 us
    pallas_call x1, Pallas kernels, shards(): pl.pallas_call(functools.partial(first_kernel, **mults), out_shape=(tile_...  3.75 us
    pallas_call x1, Pallas kernels, shards(): pl.pallas_call(functools.partial(last_kernel, scale=scale_a), out_shape=f...  2.12 us
    pallas_call x3, Pallas kernels, shards(): pl.pallas_call(functools.partial(terms_kernel, **mults), out_shape=(grams...  1.6 us
  transfers between devices with their start and end apart: 25, of which 17 were waited for; matrix products, arithmetic and copies ran while one was open for 0% of the time, Pallas kernels for 27%

profile of v2, /device:TPU:0, one launch (start us, length us, event | category | flops | bytes accessed | tf_op | source)
XLA Modules:
  0.0 72.9 jit_solution(13792574126706368439)
XLA Ops:
  0.7 3.7 %shard_map.103 = (bf16[64,64,128]{2,1,0:T(8,128)(2,1)S(1)}, f32[64,256]{1,0:T(8,128)S(1)}, f32[128,256]{1,0:T(8,128)S(1)}, f32[64,256]{1,0:T(8,128)S(1)}, f32[64...) custom-call(s32[1]{0:T(128)} %bitcast.core, ...), custom_call_target="tpu_custom_call" | custom-call | tf_op jit(solution)/shard_map/pallas_call | solution.py:382
  4.5 0.6 collective-permute-start
  5.0 1.0 %collective-permute-done = f32[128,256]{1,0:T(8,128)S(1)} collective-permute-done((f32[128,256]{1,0:T(8,128)S(1)}, f32[128,256]{1,0:T(8,128)S(1)}, u32[]{:S(2)}, u32[]{:S(2)}) %collective-permute-start) | collective-permute-done | bytes 131104 | tf_op jit(solution)/shard_map/ppermute | solution.py:334
  6.1 2.9 %collective-permute-start.1 = (f32[64,256]{1,0:T(8,128)S(1)}, f32[64,256]{1,0:T(8,128)S(1)}, u32[]{:S(2)}, u32[]{:S(2)}) collective-permute-start(f32[64,256]{1,0:T(8,128)S(1)} %get-tuple-element.214), channel_id=1, source_target_pairs={{0,4},{1,15},{2,6},{3,13},{4,8},{5,19},{6,10},{7,17},{8,12},{9,23}... | collective-permute-start | bytes 196616 | tf_op jit(solution)/shard_map/ppermute | solution.py:334
  8.9 2.5 %collective-permute-start.2 = (f32[64,256]{1,0:T(8,128)S(1)}, f32[64,256]{1,0:T(8,128)S(1)}, u32[]{:S(2)}, u32[]{:S(2)}) collective-permute-start(f32[64,256]{1,0:T(8,128)S(1)} %get-tuple-element.215), channel_id=1, source_target_pairs={{0,6},{1,5},{2,4},{3,7},{4,10},{5,9},{6,8},{7,11},{8,14},{9,13},{1... | collective-permute-start | bytes 196616 | tf_op jit(solution)/shard_map/ppermute | solution.py:334
  11.4 2.5 %collective-permute-start.3 = (f32[64,256]{1,0:T(8,128)S(1)}, f32[64,256]{1,0:T(8,128)S(1)}, u32[]{:S(2)}, u32[]{:S(2)}) collective-permute-start(f32[64,256]{1,0:T(8,128)S(1)} %get-tuple-element.213), channel_id=1, source_target_pairs={{0,12},{1,7},{2,14},{3,5},{4,16},{5,11},{6,18},{7,9},{8,20},{9,15}... | collective-permute-start | bytes 196616 | tf_op jit(solution)/shard_map/ppermute | solution.py:334
  14.0 3.6 %shard_map.104 = (bf16[64,64,128]{2,1,0:T(8,128)(2,1)S(1)}, f32[64,256]{1,0:T(8,128)S(1)}, f32[64,256]{1,0:T(8,128)S(1)}, f32[256,256]{1,0:T(8,128)S(1)}, f32[64,128,256]{2,1,0:T(8,128)S(1)}) custom-call(s32[1,4]{1,0:T(1,128)} %slot_in.7, bf16[4,64,64,128]{3,2,1,0:T(8,128)(2,1)} %tiles.7, bf16[64,64,128]{2,1,0:T(8,128)(2,1)S(1)} %get-tuple-element.107.old, ...), custom_call_target="tpu_custom_call" | custom-call | tf_op jit(solution)/shard_map/pallas_call | solution.py:422
  17.6 0.0 collective-permute-done.1
  17.6 0.0 collective-permute-done.2
  17.6 2.0 %collective-permute-done.3 = f32[64,256]{1,0:T(8,128)S(1)} collective-permute-done((f32[64,256]{1,0:T(8,128)S(1)}, f32[64,256]{1,0:T(8,128)S(1)}, u32[]{:S(2)}, u32[]{:S(2)}) %collective-permute-start.3) | collective-permute-done | bytes 65568 | tf_op jit(solution)/shard_map/ppermute | solution.py:334
  19.6 0.1 collective-permute-start.4
  19.7 0.4 collective-permute-start.5
  20.1 0.2 collective-permute-start.7
  20.2 0.8 %collective-permute-done.4.other = f32[128,256]{1,0:T(8,128)S(1)} collective-permute-done((f32[128,256]{1,0:T(8,128)S(1)}, f32[128,256]{1,0:T(8,128)S(1)}, u32[]{:S(2)}, u32[]{:S(2)}) %collective-permute-start.4) | collective-permute-done | bytes 131104 | tf_op jit(solution)/shard_map/ppermute | solution.py:334
  21.0 1.7 %shard_map.105 = (f32[128,256]{1,0:T(8,128)S(1)}, f32[64,256]{1,0:T(8,128)S(1)}, f32[128,256]{1,0:T(8,128)S(1)}, f32[128,256]{1,0:T(8,128)S(1)}) custom-call(s32[1]{0:T(128)} %bitcast.core, bf16[64,64,128]{2,1,0:T(8,128)(2,1)S(1)} %get-tuple-element.132.tile.old, f32[64,128,256]{2,1,0:T(8,128)S(1)} %get-tuple-element.118.z, ...), custom_call_target="tpu_custom_call" | custom-call | tf_op jit(solution)/shard_map/pallas_call | solution.py:438
  22.8 4.1 %collective-permute-done.5 = f32[64,256]{1,0:T(8,128)S(1)} collective-permute-done((f32[64,256]{1,0:T(8,128)S(1)}, f32[64,256]{1,0:T(8,128)S(1)}, u32[]{:S(2)}, u32[]{:S(2)}) %collective-permute-start.5) | collective-permute-done | bytes 65568 | tf_op jit(solution)/shard_map/ppermute | solution.py:334
  26.9 0.1 collective-permute-start.6
  27.0 0.0 collective-permute-done.7.ata_other
  27.0 0.5 shard_map.106
  27.6 0.8 %collective-permute-done.6 = f32[128,256]{1,0:T(8,128)S(1)} collective-permute-done((f32[128,256]{1,0:T(8,128)S(1)}, f32[128,256]{1,0:T(8,128)S(1)}, u32[]{:S(2)}, u32[]{:S(2)}) %collective-permute-start.6) | collective-permute-done | bytes 131104 | tf_op jit(solution)/shard_map/ppermute | solution.py:334
  28.4 0.1 collective-permute-start.10
  28.5 0.7 collective-permute-start.8
  29.2 1.2 %collective-permute-start.9 = (f32[64,256]{1,0:T(8,128)S(1)}, f32[64,256]{1,0:T(8,128)S(1)}, u32[]{:S(2)}, u32[]{:S(2)}) collective-permute-start(f32[64,256]{1,0:T(8,128)S(1)} %get-tuple-element.212), channel_id=1, source_target_pairs={{0,6},{1,5},{2,4},{3,7},{4,10},{5,9},{6,8},{7,11},{8,14},{9,13},{1... | collective-permute-start | bytes 196616 | tf_op jit(solution)/shard_map/ppermute | solution.py:334
  30.4 3.6 %shard_map.107 = (bf16[64,64,128]{2,1,0:T(8,128)(2,1)S(1)}, f32[64,256]{1,0:T(8,128)S(1)}, f32[64,256]{1,0:T(8,128)S(1)}, f32[256,256]{1,0:T(8,128)S(1)}, f32[64,128,256]{2,1,0:T(8,128)S(1)}) custom-call(s32[1,4]{1,0:T(1,128)} %slot_in.7, bf16[4,64,64,128]{3,2,1,0:T(8,128)(2,1)} %tiles.7, bf16[64,64,128]{2,1,0:T(8,128)(2,1)S(1)} %get-tuple-element.132.tile.old, ...), custom_call_target="tpu_custom_call" | custom-call | tf_op jit(solution)/shard_map/pallas_call | solution.py:422
  34.0 4.1 %collective-permute-done.10 = f32[64,256]{1,0:T(8,128)S(1)} collective-permute-done((f32[64,256]{1,0:T(8,128)S(1)}, f32[64,256]{1,0:T(8,128)S(1)}, u32[]{:S(2)}, u32[]{:S(2)}) %collective-permute-start.10) | collective-permute-done | bytes 65568 | tf_op jit(solution)/shard_map/ppermute | solution.py:334
  38.1 0.0 collective-permute-done.8
  38.1 0.0 collective-permute-done.9
  38.2 0.3 collective-permute-start.11
  38.5 0.0 collective-permute-start.12
  38.5 0.3 collective-permute-start.14
  38.7 0.8 %collective-permute-done.11.other = f32[128,256]{1,0:T(8,128)S(1)} collective-permute-done((f32[128,256]{1,0:T(8,128)S(1)}, f32[128,256]{1,0:T(8,128)S(1)}, u32[]{:S(2)}, u32[]{:S(2)}) %collective-permute-start.11) | collective-permute-done | bytes 131104 | tf_op jit(solution)/shard_map/ppermute | solution.py:334
  39.6 1.7 %shard_map.108 = (f32[128,256]{1,0:T(8,128)S(1)}, f32[64,256]{1,0:T(8,128)S(1)}, f32[128,256]{1,0:T(8,128)S(1)}, f32[128,256]{1,0:T(8,128)S(1)}) custom-call(s32[1]{0:T(128)} %bitcast.core, bf16[64,64,128]{2,1,0:T(8,128)(2,1)S(1)} %get-tuple-element.156.tile.old, f32[64,128,256]{2,1,0:T(8,128)S(1)} %get-tuple-element.143.z, ...), custom_call_target="tpu_custom_call" | custom-call | tf_op jit(solution)/shard_map/pallas_call | solution.py:438
  41.3 4.1 %collective-permute-done.12 = f32[64,256]{1,0:T(8,128)S(1)} collective-permute-done((f32[64,256]{1,0:T(8,128)S(1)}, f32[64,256]{1,0:T(8,128)S(1)}, u32[]{:S(2)}, u32[]{:S(2)}) %collective-permute-start.12) | collective-permute-done | bytes 65568 | tf_op jit(solution)/shard_map/ppermute | solution.py:334
  45.5 0.1 collective-permute-start.13
  45.5 0.0 collective-permute-done.14.ata_other
  45.6 0.5 shard_map.109
  46.1 0.8 %collective-permute-done.13 = f32[128,256]{1,0:T(8,128)S(1)} collective-permute-done((f32[128,256]{1,0:T(8,128)S(1)}, f32[128,256]{1,0:T(8,128)S(1)}, u32[]{:S(2)}, u32[]{:S(2)}) %collective-permute-start.13) | collective-permute-done | bytes 131104 | tf_op jit(solution)/shard_map/ppermute | solution.py:334
  46.9 0.1 collective-permute-start.15
  47.0 1.6 %collective-permute-start.16 = (f32[64,256]{1,0:T(8,128)S(1)}, f32[64,256]{1,0:T(8,128)S(1)}, u32[]{:S(2)}, u32[]{:S(2)}) collective-permute-start(f32[64,256]{1,0:T(8,128)S(1)} %get-tuple-element.209), channel_id=1, source_target_pairs={{0,6},{1,5},{2,4},{3,7},{4,10},{5,9},{6,8},{7,11},{8,14},{9,13},{1... | collective-permute-start | bytes 196616 | tf_op jit(solution)/shard_map/ppermute | solution.py:334
  48.7 0.5 collective-permute-start.17
  49.2 3.6 %shard_map.110 = (bf16[64,64,128]{2,1,0:T(8,128)(2,1)S(1)}, f32[64,256]{1,0:T(8,128)S(1)}, f32[64,256]{1,0:T(8,128)S(1)}, f32[256,256]{1,0:T(8,128)S(1)}, f32[64,128,256]{2,1,0:T(8,128)S(1)}) custom-call(s32[1,4]{1,0:T(1,128)} %slot_in.7, bf16[4,64,64,128]{3,2,1,0:T(8,128)(2,1)} %tiles.7, bf16[64,64,128]{2,1,0:T(8,128)(2,1)S(1)} %get-tuple-element.156.tile.old, ...), custom_call_target="tpu_custom_call" | custom-call | tf_op jit(solution)/shard_map/pallas_call | solution.py:422
  52.8 1.9 %collective-permute-done.15 = f32[64,256]{1,0:T(8,128)S(1)} collective-permute-done((f32[64,256]{1,0:T(8,128)S(1)}, f32[64,256]{1,0:T(8,128)S(1)}, u32[]{:S(2)}, u32[]{:S(2)}) %collective-permute-start.15) | collective-permute-done | bytes 65568 | tf_op jit(solution)/shard_map/ppermute | solution.py:334
  54.7 1.3 %collective-permute-done.16 = f32[64,256]{1,0:T(8,128)S(1)} collective-permute-done((f32[64,256]{1,0:T(8,128)S(1)}, f32[64,256]{1,0:T(8,128)S(1)}, u32[]{:S(2)}, u32[]{:S(2)}) %collective-permute-start.16) | collective-permute-done | bytes 65568 | tf_op jit(solution)/shard_map/ppermute | solution.py:334
  56.0 1.0 %collective-permute-done.17 = f32[64,256]{1,0:T(8,128)S(1)} collective-permute-done((f32[64,256]{1,0:T(8,128)S(1)}, f32[64,256]{1,0:T(8,128)S(1)}, u32[]{:S(2)}, u32[]{:S(2)}) %collective-permute-start.17) | collective-permute-done | bytes 65568 | tf_op jit(solution)/shard_map/ppermute | solution.py:334
  57.1 0.1 collective-permute-start.18
  57.2 0.1 collective-permute-start.19
  57.3 0.4 collective-permute-start.21
  57.7 0.8 %collective-permute-done.18.other = f32[128,256]{1,0:T(8,128)S(1)} collective-permute-done((f32[128,256]{1,0:T(8,128)S(1)}, f32[128,256]{1,0:T(8,128)S(1)}, u32[]{:S(2)}, u32[]{:S(2)}) %collective-permute-start.18) | collective-permute-done | bytes 131104 | tf_op jit(solution)/shard_map/ppermute | solution.py:334
  58.5 1.7 %shard_map.111 = (f32[128,256]{1,0:T(8,128)S(1)}, f32[64,256]{1,0:T(8,128)S(1)}, f32[128,256]{1,0:T(8,128)S(1)}, f32[128,256]{1,0:T(8,128)S(1)}) custom-call(s32[1]{0:T(128)} %bitcast.core, bf16[64,64,128]{2,1,0:T(8,128)(2,1)S(1)} %get-tuple-element.181.tile.old, f32[64,128,256]{2,1,0:T(8,128)S(1)} %get-tuple-element.167.z, ...), custom_call_target="tpu_custom_call" | custom-call | tf_op jit(solution)/shard_map/pallas_call | solution.py:438
  60.3 4.1 %collective-permute-done.19 = f32[64,256]{1,0:T(8,128)S(1)} collective-permute-done((f32[64,256]{1,0:T(8,128)S(1)}, f32[64,256]{1,0:T(8,128)S(1)}, u32[]{:S(2)}, u32[]{:S(2)}) %collective-permute-start.19) | collective-permute-done | bytes 65568 | tf_op jit(solution)/shard_map/ppermute | solution.py:334
  64.4 0.1 collective-permute-start.20
  64.5 0.0 collective-permute-done.21.ata_other
  64.5 0.5 shard_map.112
  65.1 0.8 %collective-permute-done.20 = f32[128,256]{1,0:T(8,128)S(1)} collective-permute-done((f32[128,256]{1,0:T(8,128)S(1)}, f32[128,256]{1,0:T(8,128)S(1)}, u32[]{:S(2)}, u32[]{:S(2)}) %collective-permute-start.20) | collective-permute-done | bytes 131104 | tf_op jit(solution)/shard_map/ppermute | solution.py:334
  65.9 0.8 %collective-permute-start.23 = (f32[128,256]{1,0:T(8,128)S(1)}, f32[128,256]{1,0:T(8,128)S(1)}, u32[]{:S(2)}, u32[]{:S(2)}) collective-permute-start(f32[128,256]{1,0:T(8,128)S(1)} %fusion.6.total), channel_id=1, source_target_pairs={{0,2},{1,3},{2,0},{3,1},{4,6},{5,7},{6,4},{7,5},{8,10},{9,11},{10,... | collective-permute-start | bytes 393224 | tf_op jit(solution)/shard_map/ppermute | solution.py:334
  66.7 0.0 collective-permute-start.22
  66.7 1.4 %collective-permute-start.24 = (f32[64,256]{1,0:T(8,128)S(1)}, f32[64,256]{1,0:T(8,128)S(1)}, u32[]{:S(2)}, u32[]{:S(2)}) collective-permute-start(f32[64,256]{1,0:T(8,128)S(1)} %slice.28), channel_id=1, source_target_pairs={{0,3},{1,2},{2,1},{3,0},{4,7},{5,6},{6,5},{7,4},{8,11},{9,10},{10,... | collective-permute-start | bytes 196616 | tf_op jit(solution)/shard_map/ppermute | solution.py:334
  68.1 2.1 %shard_map.113 = f32[64,256]{1,0:T(8,128)} custom-call(bf16[64,64,128]{2,1,0:T(8,128)(2,1)S(1)} %get-tuple-element.181.tile.old, f32[64,256]{1,0:T(8,128)S(1)} %get-tuple-element.182.a, f32[64,256]{1,0:T(8,128)S(1)} %get-tuple-element.183.va, f32[128,256]{1,0:T(8,128)S(1)} %get-tuple-element.184.b, f32[64,256]{1,0:T(8,128)S(1)} %get-tuple-element.185.c, ...), custom_call_target="tpu_custom_call" | custom-call | tf_op jit(solution)/shard_map/pallas_call | solution.py:450
  70.2 0.0 collective-permute-done.22.beside
  70.2 1.9 %collective-permute-done.24 = f32[64,256]{1,0:T(8,128)S(1)} collective-permute-done((f32[64,256]{1,0:T(8,128)S(1)}, f32[64,256]{1,0:T(8,128)S(1)}, u32[]{:S(2)}, u32[]{:S(2)}) %collective-permute-start.24) | collective-permute-done | bytes 65568 | tf_op jit(solution)/shard_map/ppermute | solution.py:334
  72.1 0.1 collective-permute-done.23
  72.2 0.7 shard_map.114
  (22 shorter events, 0.4 us)
Async XLA Ops:
  4.5 1.5 %collective-permute-start = (f32[128,256]{1,0:T(8,128)S(1)}, f32[128,256]{1,0:T(8,128)S(1)}, u32[]{:S(2)}, u32[]{:S(2)}) collective-permute-start(f32[128,256]{1,0:T(8,128)S(1)} %pad_add_fusion.3), channel_id=1, source_target_pairs={{0,1},{1,0},{2,3},{3,2},{4,5},{5,4},{6,7},{7,6},{8,9},{9,8},{10,11... | collective-permute-start | bytes 393224 | tf_op jit(solution)/shard_map/ppermute | solution.py:334
  6.1 11.5 %collective-permute-start.1 = (f32[64,256]{1,0:T(8,128)S(1)}, f32[64,256]{1,0:T(8,128)S(1)}, u32[]{:S(2)}, u32[]{:S(2)}) collective-permute-start(f32[64,256]{1,0:T(8,128)S(1)} %get-tuple-element.214), channel_id=1, source_target_pairs={{0,4},{1,15},{2,6},{3,13},{4,8},{5,19},{6,10},{7,17},{8,12},{9,23}... | collective-permute-start | bytes 196616 | tf_op jit(solution)/shard_map/ppermute | solution.py:334
  8.9 8.6 %collective-permute-start.2 = (f32[64,256]{1,0:T(8,128)S(1)}, f32[64,256]{1,0:T(8,128)S(1)}, u32[]{:S(2)}, u32[]{:S(2)}) collective-permute-start(f32[64,256]{1,0:T(8,128)S(1)} %get-tuple-element.215), channel_id=1, source_target_pairs={{0,6},{1,5},{2,4},{3,7},{4,10},{5,9},{6,8},{7,11},{8,14},{9,13},{1... | collective-permute-start | bytes 196616 | tf_op jit(solution)/shard_map/ppermute | solution.py:334
  11.4 8.1 %collective-permute-start.3 = (f32[64,256]{1,0:T(8,128)S(1)}, f32[64,256]{1,0:T(8,128)S(1)}, u32[]{:S(2)}, u32[]{:S(2)}) collective-permute-start(f32[64,256]{1,0:T(8,128)S(1)} %get-tuple-element.213), channel_id=1, source_target_pairs={{0,12},{1,7},{2,14},{3,5},{4,16},{5,11},{6,18},{7,9},{8,20},{9,15}... | collective-permute-start | bytes 196616 | tf_op jit(solution)/shard_map/ppermute | solution.py:334
  19.6 1.4 %collective-permute-start.4 = (f32[128,256]{1,0:T(8,128)S(1)}, f32[128,256]{1,0:T(8,128)S(1)}, u32[]{:S(2)}, u32[]{:S(2)}) collective-permute-start(f32[128,256]{1,0:T(8,128)S(1)} %pad_maximum_fusion.mine), channel_id=1, source_target_pairs={{0,1},{1,0},{2,3},{3,2},{4,5},{5,4},{6,7},{7,6},{8,9},{9,8},{10,11... | collective-permute-start | bytes 393224 | tf_op jit(solution)/shard_map/ppermute | solution.py:334
  19.7 7.2 %collective-permute-start.5 = (f32[64,256]{1,0:T(8,128)S(1)}, f32[64,256]{1,0:T(8,128)S(1)}, u32[]{:S(2)}, u32[]{:S(2)}) collective-permute-start(f32[64,256]{1,0:T(8,128)S(1)} %get-tuple-element.125), channel_id=1, source_target_pairs={{0,4},{1,5},{2,14},{3,15},{4,8},{5,9},{6,18},{7,19},{8,12},{9,13},... | collective-permute-start | bytes 196616 | tf_op jit(solution)/shard_map/ppermute | solution.py:334
  20.1 6.9 %collective-permute-start.7 = (f32[256,256]{1,0:T(8,128)S(1)}, f32[256,256]{1,0:T(8,128)S(1)}, u32[]{:S(2)}, u32[]{:S(2)}) collective-permute-start(f32[256,256]{1,0:T(8,128)S(1)} %get-tuple-element.127.ata), channel_id=1, source_target_pairs={{0,1},{1,0},{2,3},{3,2},{4,5},{5,4},{6,7},{7,6},{8,9},{9,8},{10,11... | collective-permute-start | bytes 786440 | tf_op jit(solution)/shard_map/ppermute | solution.py:334
  26.9 1.4 %collective-permute-start.6 = (f32[128,256]{1,0:T(8,128)S(1)}, f32[128,256]{1,0:T(8,128)S(1)}, u32[]{:S(2)}, u32[]{:S(2)}) collective-permute-start(f32[128,256]{1,0:T(8,128)S(1)} %pad_add_fusion.2), channel_id=1, source_target_pairs={{0,1},{1,0},{2,3},{3,2},{4,5},{5,4},{6,7},{7,6},{8,9},{9,8},{10,11... | collective-permute-start | bytes 393224 | tf_op jit(solution)/shard_map/ppermute | solution.py:334
  28.4 9.7 %collective-permute-start.10 = (f32[64,256]{1,0:T(8,128)S(1)}, f32[64,256]{1,0:T(8,128)S(1)}, u32[]{:S(2)}, u32[]{:S(2)}) collective-permute-start(f32[64,256]{1,0:T(8,128)S(1)} %get-tuple-element.210), channel_id=1, source_target_pairs={{0,12},{1,7},{2,14},{3,5},{4,16},{5,11},{6,18},{7,9},{8,20},{9,15}... | collective-permute-start | bytes 196616 | tf_op jit(solution)/shard_map/ppermute | solution.py:334
  28.5 9.6 %collective-permute-start.8 = (f32[64,256]{1,0:T(8,128)S(1)}, f32[64,256]{1,0:T(8,128)S(1)}, u32[]{:S(2)}, u32[]{:S(2)}) collective-permute-start(f32[64,256]{1,0:T(8,128)S(1)} %get-tuple-element.211), channel_id=1, source_target_pairs={{0,4},{1,15},{2,6},{3,13},{4,8},{5,19},{6,10},{7,17},{8,12},{9,23}... | collective-permute-start | bytes 196616 | tf_op jit(solution)/shard_map/ppermute | solution.py:334
  29.2 8.9 %collective-permute-start.9 = (f32[64,256]{1,0:T(8,128)S(1)}, f32[64,256]{1,0:T(8,128)S(1)}, u32[]{:S(2)}, u32[]{:S(2)}) collective-permute-start(f32[64,256]{1,0:T(8,128)S(1)} %get-tuple-element.212), channel_id=1, source_target_pairs={{0,6},{1,5},{2,4},{3,7},{4,10},{5,9},{6,8},{7,11},{8,14},{9,13},{1... | collective-permute-start | bytes 196616 | tf_op jit(solution)/shard_map/ppermute | solution.py:334
  38.2 1.4 %collective-permute-start.11 = (f32[128,256]{1,0:T(8,128)S(1)}, f32[128,256]{1,0:T(8,128)S(1)}, u32[]{:S(2)}, u32[]{:S(2)}) collective-permute-start(f32[128,256]{1,0:T(8,128)S(1)} %pad_maximum_fusion.1.mine), channel_id=1, source_target_pairs={{0,1},{1,0},{2,3},{3,2},{4,5},{5,4},{6,7},{7,6},{8,9},{9,8},{10,11... | collective-permute-start | bytes 393224 | tf_op jit(solution)/shard_map/ppermute | solution.py:334
  38.5 7.0 %collective-permute-start.12 = (f32[64,256]{1,0:T(8,128)S(1)}, f32[64,256]{1,0:T(8,128)S(1)}, u32[]{:S(2)}, u32[]{:S(2)}) collective-permute-start(f32[64,256]{1,0:T(8,128)S(1)} %get-tuple-element.196), channel_id=1, source_target_pairs={{0,4},{1,5},{2,14},{3,15},{4,8},{5,9},{6,18},{7,19},{8,12},{9,13},... | collective-permute-start | bytes 196616 | tf_op jit(solution)/shard_map/ppermute | solution.py:334
  38.5 7.1 %collective-permute-start.14 = (f32[256,256]{1,0:T(8,128)S(1)}, f32[256,256]{1,0:T(8,128)S(1)}, u32[]{:S(2)}, u32[]{:S(2)}) collective-permute-start(f32[256,256]{1,0:T(8,128)S(1)} %get-tuple-element.151.ata), channel_id=1, source_target_pairs={{0,1},{1,0},{2,3},{3,2},{4,5},{5,4},{6,7},{7,6},{8,9},{9,8},{10,11... | collective-permute-start | bytes 786440 | tf_op jit(solution)/shard_map/ppermute | solution.py:334
  45.5 1.4 %collective-permute-start.13 = (f32[128,256]{1,0:T(8,128)S(1)}, f32[128,256]{1,0:T(8,128)S(1)}, u32[]{:S(2)}, u32[]{:S(2)}) collective-permute-start(f32[128,256]{1,0:T(8,128)S(1)} %pad_add_fusion.1), channel_id=1, source_target_pairs={{0,1},{1,0},{2,3},{3,2},{4,5},{5,4},{6,7},{7,6},{8,9},{9,8},{10,11... | collective-permute-start | bytes 393224 | tf_op jit(solution)/shard_map/ppermute | solution.py:334
  46.9 7.8 %collective-permute-start.15 = (f32[64,256]{1,0:T(8,128)S(1)}, f32[64,256]{1,0:T(8,128)S(1)}, u32[]{:S(2)}, u32[]{:S(2)}) collective-permute-start(f32[64,256]{1,0:T(8,128)S(1)} %get-tuple-element.208), channel_id=1, source_target_pairs={{0,4},{1,15},{2,6},{3,13},{4,8},{5,19},{6,10},{7,17},{8,12},{9,23}... | collective-permute-start | bytes 196616 | tf_op jit(solution)/shard_map/ppermute | solution.py:334
  47.0 9.0 %collective-permute-start.16 = (f32[64,256]{1,0:T(8,128)S(1)}, f32[64,256]{1,0:T(8,128)S(1)}, u32[]{:S(2)}, u32[]{:S(2)}) collective-permute-start(f32[64,256]{1,0:T(8,128)S(1)} %get-tuple-element.209), channel_id=1, source_target_pairs={{0,6},{1,5},{2,4},{3,7},{4,10},{5,9},{6,8},{7,11},{8,14},{9,13},{1... | collective-permute-start | bytes 196616 | tf_op jit(solution)/shard_map/ppermute | solution.py:334
  48.7 8.4 %collective-permute-start.17 = (f32[64,256]{1,0:T(8,128)S(1)}, f32[64,256]{1,0:T(8,128)S(1)}, u32[]{:S(2)}, u32[]{:S(2)}) collective-permute-start(f32[64,256]{1,0:T(8,128)S(1)} %get-tuple-element.207), channel_id=1, source_target_pairs={{0,12},{1,7},{2,14},{3,5},{4,16},{5,11},{6,18},{7,9},{8,20},{9,15}... | collective-permute-start | bytes 196616 | tf_op jit(solution)/shard_map/ppermute | solution.py:334
  57.1 1.4 %collective-permute-start.18 = (f32[128,256]{1,0:T(8,128)S(1)}, f32[128,256]{1,0:T(8,128)S(1)}, u32[]{:S(2)}, u32[]{:S(2)}) collective-permute-start(f32[128,256]{1,0:T(8,128)S(1)} %pad_maximum_fusion.2.mine), channel_id=1, source_target_pairs={{0,1},{1,0},{2,3},{3,2},{4,5},{5,4},{6,7},{7,6},{8,9},{9,8},{10,11... | collective-permute-start | bytes 393224 | tf_op jit(solution)/shard_map/ppermute | solution.py:334
  57.2 7.2 %collective-permute-start.19 = (f32[64,256]{1,0:T(8,128)S(1)}, f32[64,256]{1,0:T(8,128)S(1)}, u32[]{:S(2)}, u32[]{:S(2)}) collective-permute-start(f32[64,256]{1,0:T(8,128)S(1)} %get-tuple-element.193), channel_id=1, source_target_pairs={{0,4},{1,5},{2,14},{3,15},{4,8},{5,9},{6,18},{7,19},{8,12},{9,13},... | collective-permute-start | bytes 196616 | tf_op jit(solution)/shard_map/ppermute | solution.py:334
  57.3 7.3 %collective-permute-start.21 = (f32[256,256]{1,0:T(8,128)S(1)}, f32[256,256]{1,0:T(8,128)S(1)}, u32[]{:S(2)}, u32[]{:S(2)}) collective-permute-start(f32[256,256]{1,0:T(8,128)S(1)} %get-tuple-element.175.ata), channel_id=1, source_target_pairs={{0,1},{1,0},{2,3},{3,2},{4,5},{5,4},{6,7},{7,6},{8,9},{9,8},{10,11... | collective-permute-start | bytes 786440 | tf_op jit(solution)/shard_map/ppermute | solution.py:334
  64.4 1.4 %collective-permute-start.20 = (f32[128,256]{1,0:T(8,128)S(1)}, f32[128,256]{1,0:T(8,128)S(1)}, u32[]{:S(2)}, u32[]{:S(2)}) collective-permute-start(f32[128,256]{1,0:T(8,128)S(1)} %pad_add_fusion), channel_id=1, source_target_pairs={{0,1},{1,0},{2,3},{3,2},{4,5},{5,4},{6,7},{7,6},{8,9},{9,8},{10,11... | collective-permute-start | bytes 393224 | tf_op jit(solution)/shard_map/ppermute | solution.py:334
  65.9 6.3 %collective-permute-start.23 = (f32[128,256]{1,0:T(8,128)S(1)}, f32[128,256]{1,0:T(8,128)S(1)}, u32[]{:S(2)}, u32[]{:S(2)}) collective-permute-start(f32[128,256]{1,0:T(8,128)S(1)} %fusion.6.total), channel_id=1, source_target_pairs={{0,2},{1,3},{2,0},{3,1},{4,6},{5,7},{6,4},{7,5},{8,10},{9,11},{10,... | collective-permute-start | bytes 393224 | tf_op jit(solution)/shard_map/ppermute | solution.py:334
  66.7 3.5 %collective-permute-start.22 = (f32[64,256]{1,0:T(8,128)S(1)}, f32[64,256]{1,0:T(8,128)S(1)}, u32[]{:S(2)}, u32[]{:S(2)}) collective-permute-start(f32[64,256]{1,0:T(8,128)S(1)} %slice.28), channel_id=1, source_target_pairs={{0,1},{1,0},{2,3},{3,2},{4,5},{5,4},{6,7},{7,6},{8,9},{9,8},{10,11... | collective-permute-start | bytes 196616 | tf_op jit(solution)/shard_map/ppermute | solution.py:334
  66.7 5.4 %collective-permute-start.24 = (f32[64,256]{1,0:T(8,128)S(1)}, f32[64,256]{1,0:T(8,128)S(1)}, u32[]{:S(2)}, u32[]{:S(2)}) collective-permute-start(f32[64,256]{1,0:T(8,128)S(1)} %slice.28), channel_id=1, source_target_pairs={{0,3},{1,2},{2,1},{3,0},{4,7},{5,6},{6,5},{7,4},{8,11},{9,10},{10,... | collective-permute-start | bytes 196616 | tf_op jit(solution)/shard_map/ppermute | solution.py:334

commit v3 on v2

--- a/solution.py
+++ b/solution.py
@@ -101,7 +101,7 @@
     seen = lax.fori_loop(0, early, body, jnp.zeros((ib, a.shape[1]), jnp.float32), unroll=2)
     if midway is not None:
         midway()
-    seen = lax.fori_loop(early, kb // STEP, body, seen, unroll=2)
+    seen = lax.fori_loop(early, kb // STEP, body, seen, unroll=kb // STEP - early)
     grad = apply(a[...], bc_gram[...]) - seen
     va_new = momentum * va[...] + grad * scale
     return a[...] - step_rate * va_new, va_new
@@ -130,7 +130,7 @@
             z[at + m] = zk
         return carry
 
-    lax.fori_loop(0, new.shape[0] // STEP, body, 0, unroll=4)
+    lax.fori_loop(0, new.shape[0] // STEP, body, 0, unroll=new.shape[0] // STEP)
 
 
 def last_kernel(old, a, va, b, c, bc_gram, a_out, *, scale):
@@ -272,7 +272,7 @@
         return carry
 
     y_even[...] = slices_times_b(tile, 0, stacked)
-    lax.fori_loop(0, steps // 2, body, 0, unroll=2)
+    lax.fori_loop(0, steps // 2, body, 0, unroll=steps // 2)
     place(core, mult_b * mb[...], mult_c * mc[...], keep, send)
 
 

time: 73.1 us -> 73.3 us (level)
  Pallas kernels: 24.1 us -> 23 us
  waiting for transfers between devices: 30.6 us -> 31.7 us
    pallas_call x3, Pallas kernels: 5.19 us -> 3.87 us  [shards(): pl.pallas_call(functools.partial(gradient_kernel, **mults), out_shape=(bl...]
    ppermute x25, waiting for transfers between devices: 30.6 us -> 31.7 us  [permute(): return lax.ppermute(x, BOTH, route)]
    pallas_call x3, Pallas kernels: 10.8 us -> 11.6 us  [shards(): pl.pallas_call(functools.partial(window_kernel, scale=scale_a, stratum=s...]
  transfers between devices with their start and end apart: 25 -> 25, of which waited for: 17 -> 17; matrix products, arithmetic and copies ran while one was open for 0% -> 0% of each run, Pallas kernels for 27% -> 25%
where the time goes in v3:
time: 73.3 us; the launch traced here: 72.9 us
  waiting for transfers between devices  31.7 us (43%)
  Pallas kernels  23 us (31%)
  starting transfers between devices  16.9 us (23%)
  between operations  0.96 us (1%)
    ppermute x25, waiting for transfers between devices, permute(): return lax.ppermute(x, BOTH, route)  31.7 us
    ppermute x25, starting transfers between devices, permute(): return lax.ppermute(x, BOTH, route)  16.9 us
    pallas_call x3, Pallas kernels, shards(): pl.pallas_call(functools.partial(window_kernel, scale=scale_a, stratum=s...  11.6 us
    pallas_call x3, Pallas kernels, shards(): pl.pallas_call(functools.partial(gradient_kernel, **mults), out_shape=(bl...  3.87 us
    pallas_call x1, Pallas kernels, shards(): pl.pallas_call(functools.partial(first_kernel, **mults), out_shape=(tile_...  3.75 us
    pallas_call x3, Pallas kernels, shards(): pl.pallas_call(functools.partial(terms_kernel, **mults), out_shape=(grams...  1.61 us
  transfers between devices with their start and end apart: 25, of which 17 were waited for; matrix products, arithmetic and copies ran while one was open for 0% of the time, Pallas kernels for 25%

profile of v3, /device:TPU:0, one launch (start us, length us, event | category | flops | bytes accessed | tf_op | source)
XLA Modules:
  0.0 72.9 jit_solution(14223893715288950329)
XLA Ops:
  0.7 3.7 %shard_map.103 = (bf16[64,64,128]{2,1,0:T(8,128)(2,1)S(1)}, f32[64,256]{1,0:T(8,128)S(1)}, f32[128,256]{1,0:T(8,128)S(1)}, f32[64,256]{1,0:T(8,128)S(1)}, f32[64...) custom-call(s32[1]{0:T(128)} %bitcast.core, ...), custom_call_target="tpu_custom_call" | custom-call | tf_op jit(solution)/shard_map/pallas_call | solution.py:382
  4.5 0.6 collective-permute-start
  5.0 1.0 %collective-permute-done = f32[128,256]{1,0:T(8,128)S(1)} collective-permute-done((f32[128,256]{1,0:T(8,128)S(1)}, f32[128,256]{1,0:T(8,128)S(1)}, u32[]{:S(2)}, u32[]{:S(2)}) %collective-permute-start) | collective-permute-done | bytes 131104 | tf_op jit(solution)/shard_map/ppermute | solution.py:334
  6.1 2.9 %collective-permute-start.1 = (f32[64,256]{1,0:T(8,128)S(1)}, f32[64,256]{1,0:T(8,128)S(1)}, u32[]{:S(2)}, u32[]{:S(2)}) collective-permute-start(f32[64,256]{1,0:T(8,128)S(1)} %get-tuple-element.214), channel_id=1, source_target_pairs={{0,4},{1,15},{2,6},{3,13},{4,8},{5,19},{6,10},{7,17},{8,12},{9,23}... | collective-permute-start | bytes 196616 | tf_op jit(solution)/shard_map/ppermute | solution.py:334
  8.9 2.5 %collective-permute-start.2 = (f32[64,256]{1,0:T(8,128)S(1)}, f32[64,256]{1,0:T(8,128)S(1)}, u32[]{:S(2)}, u32[]{:S(2)}) collective-permute-start(f32[64,256]{1,0:T(8,128)S(1)} %get-tuple-element.215), channel_id=1, source_target_pairs={{0,6},{1,5},{2,4},{3,7},{4,10},{5,9},{6,8},{7,11},{8,14},{9,13},{1... | collective-permute-start | bytes 196616 | tf_op jit(solution)/shard_map/ppermute | solution.py:334
  11.5 2.5 %collective-permute-start.3 = (f32[64,256]{1,0:T(8,128)S(1)}, f32[64,256]{1,0:T(8,128)S(1)}, u32[]{:S(2)}, u32[]{:S(2)}) collective-permute-start(f32[64,256]{1,0:T(8,128)S(1)} %get-tuple-element.213), channel_id=1, source_target_pairs={{0,12},{1,7},{2,14},{3,5},{4,16},{5,11},{6,18},{7,9},{8,20},{9,15}... | collective-permute-start | bytes 196616 | tf_op jit(solution)/shard_map/ppermute | solution.py:334
  14.0 3.9 %shard_map.104 = (bf16[64,64,128]{2,1,0:T(8,128)(2,1)S(1)}, f32[64,256]{1,0:T(8,128)S(1)}, f32[64,256]{1,0:T(8,128)S(1)}, f32[256,256]{1,0:T(8,128)S(1)}, f32[64,128,256]{2,1,0:T(8,128)S(1)}) custom-call(s32[1,4]{1,0:T(1,128)} %slot_in.7, bf16[4,64,64,128]{3,2,1,0:T(8,128)(2,1)} %tiles.7, bf16[64,64,128]{2,1,0:T(8,128)(2,1)S(1)} %get-tuple-element.107.old, ...), custom_call_target="tpu_custom_call" | custom-call | tf_op jit(solution)/shard_map/pallas_call | solution.py:422
  17.8 0.0 collective-permute-done.1
  17.8 0.0 collective-permute-done.2
  17.9 1.7 %collective-permute-done.3 = f32[64,256]{1,0:T(8,128)S(1)} collective-permute-done((f32[64,256]{1,0:T(8,128)S(1)}, f32[64,256]{1,0:T(8,128)S(1)}, u32[]{:S(2)}, u32[]{:S(2)}) %collective-permute-start.3) | collective-permute-done | bytes 65568 | tf_op jit(solution)/shard_map/ppermute | solution.py:334
  19.6 0.1 collective-permute-start.4
  19.7 0.4 collective-permute-start.5
  20.1 0.2 collective-permute-start.7
  20.2 0.8 %collective-permute-done.4.other = f32[128,256]{1,0:T(8,128)S(1)} collective-permute-done((f32[128,256]{1,0:T(8,128)S(1)}, f32[128,256]{1,0:T(8,128)S(1)}, u32[]{:S(2)}, u32[]{:S(2)}) %collective-permute-start.4) | collective-permute-done | bytes 131104 | tf_op jit(solution)/shard_map/ppermute | solution.py:334
  21.0 1.3 %shard_map.105 = (f32[128,256]{1,0:T(8,128)S(1)}, f32[64,256]{1,0:T(8,128)S(1)}, f32[128,256]{1,0:T(8,128)S(1)}, f32[128,256]{1,0:T(8,128)S(1)}) custom-call(s32[1]{0:T(128)} %bitcast.core, bf16[64,64,128]{2,1,0:T(8,128)(2,1)S(1)} %get-tuple-element.132.tile.old, f32[64,128,256]{2,1,0:T(8,128)S(1)} %get-tuple-element.118.z, ...), custom_call_target="tpu_custom_call" | custom-call | tf_op jit(solution)/shard_map/pallas_call | solution.py:438
  22.3 4.6 %collective-permute-done.5 = f32[64,256]{1,0:T(8,128)S(1)} collective-permute-done((f32[64,256]{1,0:T(8,128)S(1)}, f32[64,256]{1,0:T(8,128)S(1)}, u32[]{:S(2)}, u32[]{:S(2)}) %collective-permute-start.5) | collective-permute-done | bytes 65568 | tf_op jit(solution)/shard_map/ppermute | solution.py:334
  26.9 0.1 collective-permute-start.6
  27.0 0.0 collective-permute-done.7.ata_other
  27.0 0.5 shard_map.106
  27.6 0.8 %collective-permute-done.6 = f32[128,256]{1,0:T(8,128)S(1)} collective-permute-done((f32[128,256]{1,0:T(8,128)S(1)}, f32[128,256]{1,0:T(8,128)S(1)}, u32[]{:S(2)}, u32[]{:S(2)}) %collective-permute-start.6) | collective-permute-done | bytes 131104 | tf_op jit(solution)/shard_map/ppermute | solution.py:334
  28.4 0.1 collective-permute-start.10
  28.5 0.7 collective-permute-start.8
  29.2 1.2 %collective-permute-start.9 = (f32[64,256]{1,0:T(8,128)S(1)}, f32[64,256]{1,0:T(8,128)S(1)}, u32[]{:S(2)}, u32[]{:S(2)}) collective-permute-start(f32[64,256]{1,0:T(8,128)S(1)} %get-tuple-element.212), channel_id=1, source_target_pairs={{0,6},{1,5},{2,4},{3,7},{4,10},{5,9},{6,8},{7,11},{8,14},{9,13},{1... | collective-permute-start | bytes 196616 | tf_op jit(solution)/shard_map/ppermute | solution.py:334
  30.4 3.9 %shard_map.107 = (bf16[64,64,128]{2,1,0:T(8,128)(2,1)S(1)}, f32[64,256]{1,0:T(8,128)S(1)}, f32[64,256]{1,0:T(8,128)S(1)}, f32[256,256]{1,0:T(8,128)S(1)}, f32[64,128,256]{2,1,0:T(8,128)S(1)}) custom-call(s32[1,4]{1,0:T(1,128)} %slot_in.7, bf16[4,64,64,128]{3,2,1,0:T(8,128)(2,1)} %tiles.7, bf16[64,64,128]{2,1,0:T(8,128)(2,1)S(1)} %get-tuple-element.132.tile.old, ...), custom_call_target="tpu_custom_call" | custom-call | tf_op jit(solution)/shard_map/pallas_call | solution.py:422
  34.3 3.8 %collective-permute-done.10 = f32[64,256]{1,0:T(8,128)S(1)} collective-permute-done((f32[64,256]{1,0:T(8,128)S(1)}, f32[64,256]{1,0:T(8,128)S(1)}, u32[]{:S(2)}, u32[]{:S(2)}) %collective-permute-start.10) | collective-permute-done | bytes 65568 | tf_op jit(solution)/shard_map/ppermute | solution.py:334
  38.1 0.0 collective-permute-done.8
  38.1 0.0 collective-permute-done.9
  38.2 0.3 collective-permute-start.11
  38.5 0.1 collective-permute-start.12
  38.6 0.2 collective-permute-start.14
  38.8 0.8 %collective-permute-done.11.other = f32[128,256]{1,0:T(8,128)S(1)} collective-permute-done((f32[128,256]{1,0:T(8,128)S(1)}, f32[128,256]{1,0:T(8,128)S(1)}, u32[]{:S(2)}, u32[]{:S(2)}) %collective-permute-start.11) | collective-permute-done | bytes 131104 | tf_op jit(solution)/shard_map/ppermute | solution.py:334
  39.6 1.3 %shard_map.108 = (f32[128,256]{1,0:T(8,128)S(1)}, f32[64,256]{1,0:T(8,128)S(1)}, f32[128,256]{1,0:T(8,128)S(1)}, f32[128,256]{1,0:T(8,128)S(1)}) custom-call(s32[1]{0:T(128)} %bitcast.core, bf16[64,64,128]{2,1,0:T(8,128)(2,1)S(1)} %get-tuple-element.156.tile.old, f32[64,128,256]{2,1,0:T(8,128)S(1)} %get-tuple-element.143.z, ...), custom_call_target="tpu_custom_call" | custom-call | tf_op jit(solution)/shard_map/pallas_call | solution.py:438
  40.9 4.6 %collective-permute-done.12 = f32[64,256]{1,0:T(8,128)S(1)} collective-permute-done((f32[64,256]{1,0:T(8,128)S(1)}, f32[64,256]{1,0:T(8,128)S(1)}, u32[]{:S(2)}, u32[]{:S(2)}) %collective-permute-start.12) | collective-permute-done | bytes 65568 | tf_op jit(solution)/shard_map/ppermute | solution.py:334
  45.5 0.1 collective-permute-start.13
  45.6 0.0 collective-permute-done.14.ata_other
  45.6 0.5 shard_map.109
  46.1 0.8 %collective-permute-done.13 = f32[128,256]{1,0:T(8,128)S(1)} collective-permute-done((f32[128,256]{1,0:T(8,128)S(1)}, f32[128,256]{1,0:T(8,128)S(1)}, u32[]{:S(2)}, u32[]{:S(2)}) %collective-permute-start.13) | collective-permute-done | bytes 131104 | tf_op jit(solution)/shard_map/ppermute | solution.py:334
  47.0 0.1 collective-permute-start.15
  47.0 1.6 %collective-permute-start.16 = (f32[64,256]{1,0:T(8,128)S(1)}, f32[64,256]{1,0:T(8,128)S(1)}, u32[]{:S(2)}, u32[]{:S(2)}) collective-permute-start(f32[64,256]{1,0:T(8,128)S(1)} %get-tuple-element.209), channel_id=1, source_target_pairs={{0,6},{1,5},{2,4},{3,7},{4,10},{5,9},{6,8},{7,11},{8,14},{9,13},{1... | collective-permute-start | bytes 196616 | tf_op jit(solution)/shard_map/ppermute | solution.py:334
  48.7 0.5 collective-permute-start.17
  49.2 3.9 %shard_map.110 = (bf16[64,64,128]{2,1,0:T(8,128)(2,1)S(1)}, f32[64,256]{1,0:T(8,128)S(1)}, f32[64,256]{1,0:T(8,128)S(1)}, f32[256,256]{1,0:T(8,128)S(1)}, f32[64,128,256]{2,1,0:T(8,128)S(1)}) custom-call(s32[1,4]{1,0:T(1,128)} %slot_in.7, bf16[4,64,64,128]{3,2,1,0:T(8,128)(2,1)} %tiles.7, bf16[64,64,128]{2,1,0:T(8,128)(2,1)S(1)} %get-tuple-element.156.tile.old, ...), custom_call_target="tpu_custom_call" | custom-call | tf_op jit(solution)/shard_map/pallas_call | solution.py:422
  53.1 1.5 %collective-permute-done.15 = f32[64,256]{1,0:T(8,128)S(1)} collective-permute-done((f32[64,256]{1,0:T(8,128)S(1)}, f32[64,256]{1,0:T(8,128)S(1)}, u32[]{:S(2)}, u32[]{:S(2)}) %collective-permute-start.15) | collective-permute-done | bytes 65568 | tf_op jit(solution)/shard_map/ppermute | solution.py:334
  54.6 1.4 %collective-permute-done.16 = f32[64,256]{1,0:T(8,128)S(1)} collective-permute-done((f32[64,256]{1,0:T(8,128)S(1)}, f32[64,256]{1,0:T(8,128)S(1)}, u32[]{:S(2)}, u32[]{:S(2)}) %collective-permute-start.16) | collective-permute-done | bytes 65568 | tf_op jit(solution)/shard_map/ppermute | solution.py:334
  56.1 1.0 %collective-permute-done.17 = f32[64,256]{1,0:T(8,128)S(1)} collective-permute-done((f32[64,256]{1,0:T(8,128)S(1)}, f32[64,256]{1,0:T(8,128)S(1)}, u32[]{:S(2)}, u32[]{:S(2)}) %collective-permute-start.17) | collective-permute-done | bytes 65568 | tf_op jit(solution)/shard_map/ppermute | solution.py:334
  57.1 0.1 collective-permute-start.18
  57.2 0.1 collective-permute-start.19
  57.3 0.4 collective-permute-start.21
  57.7 0.8 %collective-permute-done.18.other = f32[128,256]{1,0:T(8,128)S(1)} collective-permute-done((f32[128,256]{1,0:T(8,128)S(1)}, f32[128,256]{1,0:T(8,128)S(1)}, u32[]{:S(2)}, u32[]{:S(2)}) %collective-permute-start.18) | collective-permute-done | bytes 131104 | tf_op jit(solution)/shard_map/ppermute | solution.py:334
  58.5 1.3 %shard_map.111 = (f32[128,256]{1,0:T(8,128)S(1)}, f32[64,256]{1,0:T(8,128)S(1)}, f32[128,256]{1,0:T(8,128)S(1)}, f32[128,256]{1,0:T(8,128)S(1)}) custom-call(s32[1]{0:T(128)} %bitcast.core, bf16[64,64,128]{2,1,0:T(8,128)(2,1)S(1)} %get-tuple-element.181.tile.old, f32[64,128,256]{2,1,0:T(8,128)S(1)} %get-tuple-element.167.z, ...), custom_call_target="tpu_custom_call" | custom-call | tf_op jit(solution)/shard_map/pallas_call | solution.py:438
  59.8 4.6 %collective-permute-done.19 = f32[64,256]{1,0:T(8,128)S(1)} collective-permute-done((f32[64,256]{1,0:T(8,128)S(1)}, f32[64,256]{1,0:T(8,128)S(1)}, u32[]{:S(2)}, u32[]{:S(2)}) %collective-permute-start.19) | collective-permute-done | bytes 65568 | tf_op jit(solution)/shard_map/ppermute | solution.py:334
  64.4 0.1 collective-permute-start.20
  64.5 0.0 collective-permute-done.21.ata_other
  64.5 0.5 shard_map.112
  65.1 0.8 %collective-permute-done.20 = f32[128,256]{1,0:T(8,128)S(1)} collective-permute-done((f32[128,256]{1,0:T(8,128)S(1)}, f32[128,256]{1,0:T(8,128)S(1)}, u32[]{:S(2)}, u32[]{:S(2)}) %collective-permute-start.20) | collective-permute-done | bytes 131104 | tf_op jit(solution)/shard_map/ppermute | solution.py:334
  65.9 0.8 %collective-permute-start.23 = (f32[128,256]{1,0:T(8,128)S(1)}, f32[128,256]{1,0:T(8,128)S(1)}, u32[]{:S(2)}, u32[]{:S(2)}) collective-permute-start(f32[128,256]{1,0:T(8,128)S(1)} %fusion.6.total), channel_id=1, source_target_pairs={{0,2},{1,3},{2,0},{3,1},{4,6},{5,7},{6,4},{7,5},{8,10},{9,11},{10,... | collective-permute-start | bytes 393224 | tf_op jit(solution)/shard_map/ppermute | solution.py:334
  66.7 0.0 collective-permute-start.22
  66.7 1.4 %collective-permute-start.24 = (f32[64,256]{1,0:T(8,128)S(1)}, f32[64,256]{1,0:T(8,128)S(1)}, u32[]{:S(2)}, u32[]{:S(2)}) collective-permute-start(f32[64,256]{1,0:T(8,128)S(1)} %slice.28), channel_id=1, source_target_pairs={{0,3},{1,2},{2,1},{3,0},{4,7},{5,6},{6,5},{7,4},{8,11},{9,10},{10,... | collective-permute-start | bytes 196616 | tf_op jit(solution)/shard_map/ppermute | solution.py:334
  68.1 1.4 %shard_map.113 = f32[64,256]{1,0:T(8,128)} custom-call(bf16[64,64,128]{2,1,0:T(8,128)(2,1)S(1)} %get-tuple-element.181.tile.old, f32[64,256]{1,0:T(8,128)S(1)} %get-tuple-element.182.a, f32[64,256]{1,0:T(8,128)S(1)} %get-tuple-element.183.va, f32[128,256]{1,0:T(8,128)S(1)} %get-tuple-element.184.b, f32[64,256]{1,0:T(8,128)S(1)} %get-tuple-element.185.c, ...), custom_call_target="tpu_custom_call" | custom-call | tf_op jit(solution)/shard_map/pallas_call | solution.py:450
  69.5 0.0 collective-permute-done.22.beside
  69.5 2.6 %collective-permute-done.24 = f32[64,256]{1,0:T(8,128)S(1)} collective-permute-done((f32[64,256]{1,0:T(8,128)S(1)}, f32[64,256]{1,0:T(8,128)S(1)}, u32[]{:S(2)}, u32[]{:S(2)}) %collective-permute-start.24) | collective-permute-done | bytes 65568 | tf_op jit(solution)/shard_map/ppermute | solution.py:334
  72.1 0.1 collective-permute-done.23
  72.2 0.7 shard_map.114
  (22 shorter events, 0.4 us)
Async XLA Ops:
  4.5 1.5 %collective-permute-start = (f32[128,256]{1,0:T(8,128)S(1)}, f32[128,256]{1,0:T(8,128)S(1)}, u32[]{:S(2)}, u32[]{:S(2)}) collective-permute-start(f32[128,256]{1,0:T(8,128)S(1)} %pad_add_fusion.3), channel_id=1, source_target_pairs={{0,1},{1,0},{2,3},{3,2},{4,5},{5,4},{6,7},{7,6},{8,9},{9,8},{10,11... | collective-permute-start | bytes 393224 | tf_op jit(solution)/shard_map/ppermute | solution.py:334
  6.1 11.8 %collective-permute-start.1 = (f32[64,256]{1,0:T(8,128)S(1)}, f32[64,256]{1,0:T(8,128)S(1)}, u32[]{:S(2)}, u32[]{:S(2)}) collective-permute-start(f32[64,256]{1,0:T(8,128)S(1)} %get-tuple-element.214), channel_id=1, source_target_pairs={{0,4},{1,15},{2,6},{3,13},{4,8},{5,19},{6,10},{7,17},{8,12},{9,23}... | collective-permute-start | bytes 196616 | tf_op jit(solution)/shard_map/ppermute | solution.py:334
  8.9 8.9 %collective-permute-start.2 = (f32[64,256]{1,0:T(8,128)S(1)}, f32[64,256]{1,0:T(8,128)S(1)}, u32[]{:S(2)}, u32[]{:S(2)}) collective-permute-start(f32[64,256]{1,0:T(8,128)S(1)} %get-tuple-element.215), channel_id=1, source_target_pairs={{0,6},{1,5},{2,4},{3,7},{4,10},{5,9},{6,8},{7,11},{8,14},{9,13},{1... | collective-permute-start | bytes 196616 | tf_op jit(solution)/shard_map/ppermute | solution.py:334
  11.5 8.1 %collective-permute-start.3 = (f32[64,256]{1,0:T(8,128)S(1)}, f32[64,256]{1,0:T(8,128)S(1)}, u32[]{:S(2)}, u32[]{:S(2)}) collective-permute-start(f32[64,256]{1,0:T(8,128)S(1)} %get-tuple-element.213), channel_id=1, source_target_pairs={{0,12},{1,7},{2,14},{3,5},{4,16},{5,11},{6,18},{7,9},{8,20},{9,15}... | collective-permute-start | bytes 196616 | tf_op jit(solution)/shard_map/ppermute | solution.py:334
  19.6 1.4 %collective-permute-start.4 = (f32[128,256]{1,0:T(8,128)S(1)}, f32[128,256]{1,0:T(8,128)S(1)}, u32[]{:S(2)}, u32[]{:S(2)}) collective-permute-start(f32[128,256]{1,0:T(8,128)S(1)} %pad_maximum_fusion.mine), channel_id=1, source_target_pairs={{0,1},{1,0},{2,3},{3,2},{4,5},{5,4},{6,7},{7,6},{8,9},{9,8},{10,11... | collective-permute-start | bytes 393224 | tf_op jit(solution)/shard_map/ppermute | solution.py:334
  19.7 7.2 %collective-permute-start.5 = (f32[64,256]{1,0:T(8,128)S(1)}, f32[64,256]{1,0:T(8,128)S(1)}, u32[]{:S(2)}, u32[]{:S(2)}) collective-permute-start(f32[64,256]{1,0:T(8,128)S(1)} %get-tuple-element.125), channel_id=1, source_target_pairs={{0,4},{1,5},{2,14},{3,15},{4,8},{5,9},{6,18},{7,19},{8,12},{9,13},... | collective-permute-start | bytes 196616 | tf_op jit(solution)/shard_map/ppermute | solution.py:334
  20.1 6.9 %collective-permute-start.7 = (f32[256,256]{1,0:T(8,128)S(1)}, f32[256,256]{1,0:T(8,128)S(1)}, u32[]{:S(2)}, u32[]{:S(2)}) collective-permute-start(f32[256,256]{1,0:T(8,128)S(1)} %get-tuple-element.127.ata), channel_id=1, source_target_pairs={{0,1},{1,0},{2,3},{3,2},{4,5},{5,4},{6,7},{7,6},{8,9},{9,8},{10,11... | collective-permute-start | bytes 786440 | tf_op jit(solution)/shard_map/ppermute | solution.py:334
  26.9 1.4 %collective-permute-start.6 = (f32[128,256]{1,0:T(8,128)S(1)}, f32[128,256]{1,0:T(8,128)S(1)}, u32[]{:S(2)}, u32[]{:S(2)}) collective-permute-start(f32[128,256]{1,0:T(8,128)S(1)} %pad_add_fusion.2), channel_id=1, source_target_pairs={{0,1},{1,0},{2,3},{3,2},{4,5},{5,4},{6,7},{7,6},{8,9},{9,8},{10,11... | collective-permute-start | bytes 393224 | tf_op jit(solution)/shard_map/ppermute | solution.py:334
  28.4 9.7 %collective-permute-start.10 = (f32[64,256]{1,0:T(8,128)S(1)}, f32[64,256]{1,0:T(8,128)S(1)}, u32[]{:S(2)}, u32[]{:S(2)}) collective-permute-start(f32[64,256]{1,0:T(8,128)S(1)} %get-tuple-element.210), channel_id=1, source_target_pairs={{0,12},{1,7},{2,14},{3,5},{4,16},{5,11},{6,18},{7,9},{8,20},{9,15}... | collective-permute-start | bytes 196616 | tf_op jit(solution)/shard_map/ppermute | solution.py:334
  28.5 9.6 %collective-permute-start.8 = (f32[64,256]{1,0:T(8,128)S(1)}, f32[64,256]{1,0:T(8,128)S(1)}, u32[]{:S(2)}, u32[]{:S(2)}) collective-permute-start(f32[64,256]{1,0:T(8,128)S(1)} %get-tuple-element.211), channel_id=1, source_target_pairs={{0,4},{1,15},{2,6},{3,13},{4,8},{5,19},{6,10},{7,17},{8,12},{9,23}... | collective-permute-start | bytes 196616 | tf_op jit(solution)/shard_map/ppermute | solution.py:334
  29.2 8.9 %collective-permute-start.9 = (f32[64,256]{1,0:T(8,128)S(1)}, f32[64,256]{1,0:T(8,128)S(1)}, u32[]{:S(2)}, u32[]{:S(2)}) collective-permute-start(f32[64,256]{1,0:T(8,128)S(1)} %get-tuple-element.212), channel_id=1, source_target_pairs={{0,6},{1,5},{2,4},{3,7},{4,10},{5,9},{6,8},{7,11},{8,14},{9,13},{1... | collective-permute-start | bytes 196616 | tf_op jit(solution)/shard_map/ppermute | solution.py:334
  38.2 1.4 %collective-permute-start.11 = (f32[128,256]{1,0:T(8,128)S(1)}, f32[128,256]{1,0:T(8,128)S(1)}, u32[]{:S(2)}, u32[]{:S(2)}) collective-permute-start(f32[128,256]{1,0:T(8,128)S(1)} %pad_maximum_fusion.1.mine), channel_id=1, source_target_pairs={{0,1},{1,0},{2,3},{3,2},{4,5},{5,4},{6,7},{7,6},{8,9},{9,8},{10,11... | collective-permute-start | bytes 393224 | tf_op jit(solution)/shard_map/ppermute | solution.py:334
  38.5 7.0 %collective-permute-start.12 = (f32[64,256]{1,0:T(8,128)S(1)}, f32[64,256]{1,0:T(8,128)S(1)}, u32[]{:S(2)}, u32[]{:S(2)}) collective-permute-start(f32[64,256]{1,0:T(8,128)S(1)} %get-tuple-element.196), channel_id=1, source_target_pairs={{0,4},{1,5},{2,14},{3,15},{4,8},{5,9},{6,18},{7,19},{8,12},{9,13},... | collective-permute-start | bytes 196616 | tf_op jit(solution)/shard_map/ppermute | solution.py:334
  38.6 7.0 %collective-permute-start.14 = (f32[256,256]{1,0:T(8,128)S(1)}, f32[256,256]{1,0:T(8,128)S(1)}, u32[]{:S(2)}, u32[]{:S(2)}) collective-permute-start(f32[256,256]{1,0:T(8,128)S(1)} %get-tuple-element.151.ata), channel_id=1, source_target_pairs={{0,1},{1,0},{2,3},{3,2},{4,5},{5,4},{6,7},{7,6},{8,9},{9,8},{10,11... | collective-permute-start | bytes 786440 | tf_op jit(solution)/shard_map/ppermute | solution.py:334
  45.5 1.4 %collective-permute-start.13 = (f32[128,256]{1,0:T(8,128)S(1)}, f32[128,256]{1,0:T(8,128)S(1)}, u32[]{:S(2)}, u32[]{:S(2)}) collective-permute-start(f32[128,256]{1,0:T(8,128)S(1)} %pad_add_fusion.1), channel_id=1, source_target_pairs={{0,1},{1,0},{2,3},{3,2},{4,5},{5,4},{6,7},{7,6},{8,9},{9,8},{10,11... | collective-permute-start | bytes 393224 | tf_op jit(solution)/shard_map/ppermute | solution.py:334
  47.0 7.6 %collective-permute-start.15 = (f32[64,256]{1,0:T(8,128)S(1)}, f32[64,256]{1,0:T(8,128)S(1)}, u32[]{:S(2)}, u32[]{:S(2)}) collective-permute-start(f32[64,256]{1,0:T(8,128)S(1)} %get-tuple-element.208), channel_id=1, source_target_pairs={{0,4},{1,15},{2,6},{3,13},{4,8},{5,19},{6,10},{7,17},{8,12},{9,23}... | collective-permute-start | bytes 196616 | tf_op jit(solution)/shard_map/ppermute | solution.py:334
  47.0 9.0 %collective-permute-start.16 = (f32[64,256]{1,0:T(8,128)S(1)}, f32[64,256]{1,0:T(8,128)S(1)}, u32[]{:S(2)}, u32[]{:S(2)}) collective-permute-start(f32[64,256]{1,0:T(8,128)S(1)} %get-tuple-element.209), channel_id=1, source_target_pairs={{0,6},{1,5},{2,4},{3,7},{4,10},{5,9},{6,8},{7,11},{8,14},{9,13},{1... | collective-permute-start | bytes 196616 | tf_op jit(solution)/shard_map/ppermute | solution.py:334
  48.7 8.4 %collective-permute-start.17 = (f32[64,256]{1,0:T(8,128)S(1)}, f32[64,256]{1,0:T(8,128)S(1)}, u32[]{:S(2)}, u32[]{:S(2)}) collective-permute-start(f32[64,256]{1,0:T(8,128)S(1)} %get-tuple-element.207), channel_id=1, source_target_pairs={{0,12},{1,7},{2,14},{3,5},{4,16},{5,11},{6,18},{7,9},{8,20},{9,15}... | collective-permute-start | bytes 196616 | tf_op jit(solution)/shard_map/ppermute | solution.py:334
  57.1 1.4 %collective-permute-start.18 = (f32[128,256]{1,0:T(8,128)S(1)}, f32[128,256]{1,0:T(8,128)S(1)}, u32[]{:S(2)}, u32[]{:S(2)}) collective-permute-start(f32[128,256]{1,0:T(8,128)S(1)} %pad_maximum_fusion.2.mine), channel_id=1, source_target_pairs={{0,1},{1,0},{2,3},{3,2},{4,5},{5,4},{6,7},{7,6},{8,9},{9,8},{10,11... | collective-permute-start | bytes 393224 | tf_op jit(solution)/shard_map/ppermute | solution.py:334
  57.2 7.2 %collective-permute-start.19 = (f32[64,256]{1,0:T(8,128)S(1)}, f32[64,256]{1,0:T(8,128)S(1)}, u32[]{:S(2)}, u32[]{:S(2)}) collective-permute-start(f32[64,256]{1,0:T(8,128)S(1)} %get-tuple-element.193), channel_id=1, source_target_pairs={{0,4},{1,5},{2,14},{3,15},{4,8},{5,9},{6,18},{7,19},{8,12},{9,13},... | collective-permute-start | bytes 196616 | tf_op jit(solution)/shard_map/ppermute | solution.py:334
  57.3 7.3 %collective-permute-start.21 = (f32[256,256]{1,0:T(8,128)S(1)}, f32[256,256]{1,0:T(8,128)S(1)}, u32[]{:S(2)}, u32[]{:S(2)}) collective-permute-start(f32[256,256]{1,0:T(8,128)S(1)} %get-tuple-element.175.ata), channel_id=1, source_target_pairs={{0,1},{1,0},{2,3},{3,2},{4,5},{5,4},{6,7},{7,6},{8,9},{9,8},{10,11... | collective-permute-start | bytes 786440 | tf_op jit(solution)/shard_map/ppermute | solution.py:334
  64.4 1.4 %collective-permute-start.20 = (f32[128,256]{1,0:T(8,128)S(1)}, f32[128,256]{1,0:T(8,128)S(1)}, u32[]{:S(2)}, u32[]{:S(2)}) collective-permute-start(f32[128,256]{1,0:T(8,128)S(1)} %pad_add_fusion), channel_id=1, source_target_pairs={{0,1},{1,0},{2,3},{3,2},{4,5},{5,4},{6,7},{7,6},{8,9},{9,8},{10,11... | collective-permute-start | bytes 393224 | tf_op jit(solution)/shard_map/ppermute | solution.py:334
  65.9 6.3 %collective-permute-start.23 = (f32[128,256]{1,0:T(8,128)S(1)}, f32[128,256]{1,0:T(8,128)S(1)}, u32[]{:S(2)}, u32[]{:S(2)}) collective-permute-start(f32[128,256]{1,0:T(8,128)S(1)} %fusion.6.total), channel_id=1, source_target_pairs={{0,2},{1,3},{2,0},{3,1},{4,6},{5,7},{6,4},{7,5},{8,10},{9,11},{10,... | collective-permute-start | bytes 393224 | tf_op jit(solution)/shard_map/ppermute | solution.py:334
  66.7 2.8 %collective-permute-start.22 = (f32[64,256]{1,0:T(8,128)S(1)}, f32[64,256]{1,0:T(8,128)S(1)}, u32[]{:S(2)}, u32[]{:S(2)}) collective-permute-start(f32[64,256]{1,0:T(8,128)S(1)} %slice.28), channel_id=1, source_target_pairs={{0,1},{1,0},{2,3},{3,2},{4,5},{5,4},{6,7},{7,6},{8,9},{9,8},{10,11... | collective-permute-start | bytes 196616 | tf_op jit(solution)/shard_map/ppermute | solution.py:334
  66.7 5.4 %collective-permute-start.24 = (f32[64,256]{1,0:T(8,128)S(1)}, f32[64,256]{1,0:T(8,128)S(1)}, u32[]{:S(2)}, u32[]{:S(2)}) collective-permute-start(f32[64,256]{1,0:T(8,128)S(1)} %slice.28), channel_id=1, source_target_pairs={{0,3},{1,2},{2,1},{3,0},{4,7},{5,6},{6,5},{7,4},{8,11},{9,10},{10,... | collective-permute-start | bytes 196616 | tf_op jit(solution)/shard_map/ppermute | solution.py:334
